TPU v7x, 128 devices: a whole 4x4x4 slice. The times are simulated.
128 devices in a mesh: tm: 32 (over x, y, z_hi), tensor: 4 (over z_lo, core).
Axes of the slice: x: 4, y: 4, z: 4 (z_hi: 2, z_lo: 2; z = z_hi * 2 + z_lo), core: 2. Of those that a mesh axis runs over, the one named last changes fastest.
Arguments:
- frames: bfloat16 [16384, 1408], P('tm'), may hold values from -6 to 6
- gain_attn: float32 [1408], replicated, may hold values from 0.25 to 1.75
- w_qkv: bfloat16 [1408, 3, 1408], P('tm', None, 'tensor')
- w_out: bfloat16 [1408, 1408], P('tensor', 'tm'), may hold values from -0.625 to 0.625
- gain_mlp: float32 [1408], replicated, may hold values from 0.25 to 1.75
- w_up: bfloat16 [1408, 6144], P('tm', 'tensor'), may hold values from -0.15625 to 0.15625
- w_down: bfloat16 [6144, 1408], P('tensor', 'tm'), may hold values from -0.078125 to 0.078125
- w_proj: bfloat16 [1408, 4096], P('tm', 'tensor'), may hold values from -0.15625 to 0.15625
- windows: int32 [256, 8], P('tm'), may hold values from 0 to 255, as said below
- pool_map: int32 [16384], P('tm'), may hold values from 0 to 15, as said below
- owners: int32 [4096, 1], P('tm'), may hold values from 0 to 31; in each aligned block of 128 rows (0 to 127, 128 to 255, ...) at most 8 rows name the same one
Outputs:
- received: bfloat16 [32, 256, 4096], P('tm', None, 'tensor')
Inputs may be any that keep to these rules, and one draw needn't show every extreme that they name: `windows`: row b lists 8 different blocks, each in the frame of block b or in the frame just before or just after it; frame f holds blocks 256 / 64 f onward. `pool_map`: in each aligned block of 64 patches every slot value is named by exactly 4 patches. `owners`: among the 128 rows of one index of tm no owner is named more than 8 times.
All inputs are finite; a program needn't handle non-finite values.
Results may differ from a plain program's by a relative error of at most 0.014.
The roundings to bfloat16 on the way count: a program that leaves them out, or rounds other values in their place, can miss the bound.
Values may be sent and summed in bfloat16 or wider, within the bound.
A program may use at most 64 MiB of HBM per device.

v0:
```python
import math

import jax
import jax.numpy as jnp
from jax import lax
from jax.sharding import PartitionSpec as P

D = 1408
HEADS = 16
PATCHES = 256
BLK = 64
WIN = 8
POOL = 4


eps = 1e-06


def with_halo(block, sides, width):
    for axis, dim in sides:
        count = lax.axis_size(axis)
        forward = [(i, i + 1) for i in range(count - 1)]
        backward = [(target, source) for source, target in forward]
        low = lax.ppermute(
            lax.slice_in_dim(block, block.shape[dim] - width, None, axis=dim), axis, forward
        )
        high = lax.ppermute(lax.slice_in_dim(block, 0, width, axis=dim), axis, backward)
        block = jnp.concatenate([low, block, high], axis=dim)
    return block


def layer_norm(values, scales):
    average = jnp.mean(values, axis=-1, keepdims=True)
    centred = values - average
    spread = jnp.mean(centred * centred, axis=-1, keepdims=True)
    return (centred * lax.rsqrt(spread + eps) * scales).astype(jnp.bfloat16)


def pool_rows(values, slot_map):
    block_count = values.shape[0] // BLK
    slot_ids = jnp.arange(BLK // POOL, dtype=jnp.int32)
    chooser = (slot_map.reshape(block_count, 1, BLK) == slot_ids[None, :, None]).astype(jnp.float32)
    summed = jnp.einsum(
        "bsp,bpd->bsd",
        chooser,
        values.reshape(block_count, BLK, values.shape[1]),
        precision=lax.Precision.HIGHEST,
    )
    return (
        (summed * (1.0 / POOL))
        .reshape(block_count * (BLK // POOL), values.shape[1])
        .astype(jnp.bfloat16)
    )


def tensor_total(term):
    return lax.psum(term.astype(jnp.bfloat16), "tensor").astype(jnp.float32)


def body(
    frames, gain_attn, w_qkv, w_out, gain_mlp, w_up, w_down, w_proj, windows, pool_map, owners
):
    row_count = frames.shape[0]
    query_blocks = row_count // BLK
    head_dim = D // HEADS
    full_qkv, full_out, full_up, full_down, full_proj = (
        lax.all_gather(w_qkv, "tm", axis=0, tiled=True),
        lax.all_gather(w_out, "tm", axis=1, tiled=True),
        lax.all_gather(w_up, "tm", axis=0, tiled=True),
        lax.all_gather(w_down, "tm", axis=1, tiled=True),
        lax.all_gather(w_proj, "tm", axis=0, tiled=True),
    )
    local_width = full_qkv.shape[2]
    heads_here = local_width // head_dim
    normed = layer_norm(frames.astype(jnp.float32), gain_attn)
    projected_qkv = jnp.dot(
        normed, full_qkv.reshape(D, 3 * local_width), preferred_element_type=jnp.float32
    ).astype(jnp.bfloat16)
    projected_qkv = projected_qkv.reshape(row_count, 3, local_width)
    keyvals = with_halo(projected_qkv[:, 1:, :], (("tm", 0),), PATCHES)
    per_frame = PATCHES // BLK
    kv_blocks = keyvals.reshape(query_blocks + 2 * per_frame, BLK, 2, heads_here, head_dim)
    local_ids = windows - (lax.axis_index("tm") * query_blocks - per_frame)
    group_size = math.gcd(query_blocks, 8)
    queries = projected_qkv[:, 0, :].reshape(
        query_blocks // group_size, group_size, BLK, heads_here, head_dim
    )
    score_scale = head_dim ** (-0.5)

    def attend_group(packed):
        query_group, id_group = packed
        picked = kv_blocks[id_group].reshape(group_size, WIN * BLK, 2, heads_here, head_dim)
        scores = (
            jnp.einsum(
                "gqhd,gkhd->ghqk", query_group, picked[:, :, 0], preferred_element_type=jnp.float32
            )
            * score_scale
        )
        row_top = jnp.max(scores, axis=-1, keepdims=True)
        expw = jnp.exp(scores - row_top)
        attn_probs = (expw / jnp.sum(expw, axis=-1, keepdims=True)).astype(jnp.bfloat16)
        return jnp.einsum(
            "ghqk,gkhd->gqhd", attn_probs, picked[:, :, 1], preferred_element_type=jnp.float32
        ).astype(jnp.bfloat16)

    attended = lax.map(
        attend_group, (queries, local_ids.reshape(query_blocks // group_size, group_size, WIN))
    ).reshape(row_count, local_width)
    mixed_term = jnp.dot(attended, full_out, preferred_element_type=jnp.float32)
    stream = frames.astype(jnp.float32) + tensor_total(mixed_term)
    hidden = layer_norm(stream, gain_mlp)
    activation = jax.nn.gelu(
        jnp.dot(hidden, full_up, preferred_element_type=jnp.float32), approximate=False
    ).astype(jnp.bfloat16)
    stream = stream + tensor_total(
        jnp.dot(activation, full_down, preferred_element_type=jnp.float32)
    )
    pooled = pool_rows(stream, pool_map)
    proj_rows = jnp.dot(pooled, full_proj, preferred_element_type=jnp.float32).astype(jnp.bfloat16)
    pooled_count = proj_rows.shape[0]
    owner_count = lax.axis_size("tm")
    capacity = 2 * pooled_count // owner_count
    owner_ids = owners[:, 0]
    owner_hits = (owner_ids[:, None] == jnp.arange(owner_count, dtype=jnp.int32)[None, :]).astype(
        jnp.int32
    )
    slot_rank = jnp.sum((jnp.cumsum(owner_hits, axis=0) - 1) * owner_hits, axis=1)
    slot_dest = owner_ids * capacity + slot_rank
    placement = (
        jnp.arange(owner_count * capacity, dtype=jnp.int32)[:, None] == slot_dest[None, :]
    ).astype(jnp.bfloat16)
    outbox = jnp.dot(placement, proj_rows, preferred_element_type=jnp.float32).astype(jnp.bfloat16)
    outbox = outbox.reshape(owner_count, capacity, proj_rows.shape[1])
    received = lax.all_to_all(outbox, "tm", split_axis=0, concat_axis=0, tiled=True)
    return received.reshape(1, owner_count * capacity, proj_rows.shape[1])


def solution(mesh):
    placed = (
        P("tm", None),
        P(),
        P("tm", None, "tensor"),
        P("tensor", "tm"),
        P(),
        P("tm", "tensor"),
        P("tensor", "tm"),
        P("tm", "tensor"),
        P("tm", None),
        P("tm"),
        P("tm", None),
    )
    return jax.shard_map(
        body, mesh=mesh, in_specs=placed, out_specs=P("tm", None, "tensor"), check_vma=False
    )
```

profile of v0, /device:TPU:0, one launch (start us, length us, event | category | flops | bytes accessed | tf_op | source)
XLA Modules:
  0.0 647.8 jit_solution(6431842312539559043)
XLA Ops:
  12.5 83.1 %all-gather.9.cloned.1.call-done = bf16[1408,3,352]{2,1,0:T(4,128)(2,1)} async-done(((bf16[44,3,352]{2,1,0:T(4,128)(2,1)}), bf16[1408,3,352]{2,1,0:T(4,128)(2,1)}) %all-gather.9.cloned.1.call-update) | async-done | bytes 2973712 | tf_op jit(solution)/shard_map/all_gather | solution.py:67
  95.6 7.7 %copy.24 = bf16[1408,3,352]{0,2,1:T(8,128)(2,1)} copy(bf16[1408,3,352]{2,1,0:T(4,128)(2,1)} %all-gather.9.cloned.1.call-done) | data formatting | bytes 5947392 | tf_op jit(solution)/shard_map/all_gather | solution.py:67
  103.3 3.9 convolution_convert_fusion.2
  108.4 2.3 collective-permute-start
  113.0 102.0 %all-gather = bf16[32,44,352]{2,1,0:T(8,128)(2,1)S(1)} all-gather(bf16[1,44,352]{2,1,0:T(8,128)(2,1)S(1)} %bitcast.53), channel_id=1, replica_groups=mesh['tm'=32,'tensor'=4] {'tm'}, dimensions={0}, use_global_device_ids=true | all-gather | bytes 1022208 | tf_op jit(solution)/shard_map/all_gather | solution.py:68
  226.6 5.5 gather_fusion
  232.1 9.4 %copy.29 = bf16[64,64,2,4,88]{4,1,0,3,2:T(8,128)(2,1)} copy(bf16[64,64,2,4,88]{4,1,3,2,0:T(8,128)(2,1)} %gather_fusion) | data formatting | bytes 11534336 | tf_op jit(solution)/shard_map/while/body/eval_jaxpr/gather | solution.py:92
  241.5 5.9 fusion.110
  247.4 6.2 copy.40
  253.6 2.6 fusion.19
  256.1 2.8 fusion.112
  259.0 6.1 copy.38
  265.1 4.4 fusion.72
  274.5 41.4 %all-reduce.3.cloned.1.call-done = bf16[512,1408]{1,0:T(8,128)(2,1)} async-done(((bf16[512,1408]{1,0:T(8,128)(2,1)}), bf16[512,1408]{1,0:T(8,128)(2,1)}) %all-reduce.3.cloned.1.call-update) | async-done | bytes 1441808 | tf_op jit(solution)/shard_map/psum | solution.py:57
  318.5 86.1 %all-gather.11.cloned.1.call-done = bf16[32,44,1536]{2,1,0:T(8,128)(2,1)} async-done(((bf16[1,44,1536]{2,1,0:T(8,128)(2,1)}), bf16[32,44,1536]{2,1,0:T(8,128)(2,1)}) %all-gather.11.cloned.1.call-update) | async-done | bytes 4325392 | tf_op jit(solution)/shard_map/all_gather | solution.py:69
  404.6 7.0 %reshape.92 = bf16[1408,1536]{1,0:T(8,128)(2,1)} reshape(bf16[32,44,1536]{2,1,0:T(8,128)(2,1)} %all-gather.11.cloned.1.call-done) | data formatting | bytes 8650752
  411.7 77.3 %all-gather.13.cloned.1.call-done = bf16[32,44,1536]{2,1,0:T(8,128)(2,1)} async-done(((bf16[1,44,1536]{2,1,0:T(8,128)(2,1)}), bf16[32,44,1536]{2,1,0:T(8,128)(2,1)}) %all-gather.13.cloned.1.call-update) | async-done | bytes 4325392 | tf_op jit(solution)/shard_map/all_gather | solution.py:70
  488.9 7.0 %reshape.94 = bf16[1408,1536]{1,0:T(8,128)(2,1)} reshape(bf16[32,44,1536]{2,1,0:T(8,128)(2,1)} %all-gather.13.cloned.1.call-done) | data formatting | bytes 8650752
  496.0 15.1 %convolution_convert_fusion = bf16[512,1408]{1,0:T(8,128)(2,1)} fusion(bf16[1408,1536]{1,0:T(8,128)(2,1)} %reshape.94, bf16[1408,1536]{1,0:T(8,128)(2,1)} %reshape.92, bf16[512,1408]{1,0:T(8,128)(2,1)S(1)} %copy-done.1, bf16[512,1408]{1,0:T(8,128)(2,1)S(1)} %copy-done, f32[1408]{0:T(1024)S(1)} %copy-done.9, f32[512]{0:T(512)S(1)} %add_rsqrt_fusion, ...), kind=kOutput, calls=%fused_computation.30 | convolution fusion | flops 4486070272 | bytes 12985856 | tf_op jit(solution)/shard_map/dot_general | solution.py:116
  511.6 54.0 %all-gather.15.cloned.1.call-done = bf16[32,44,1024]{2,1,0:T(8,128)(2,1)} async-done(((bf16[1,44,1024]{2,1,0:T(8,128)(2,1)}), bf16[32,44,1024]{2,1,0:T(8,128)(2,1)}) %all-gather.15.cloned.1.call-update) | async-done | bytes 2883600 | tf_op jit(solution)/shard_map/all_gather | solution.py:71
  565.6 5.2 reshape.96
  570.8 40.6 %all-reduce.5.cloned.1.call-done = bf16[512,1408]{1,0:T(8,128)(2,1)} async-done(((bf16[512,1408]{1,0:T(8,128)(2,1)}), bf16[512,1408]{1,0:T(8,128)(2,1)}) %all-reduce.5.cloned.1.call-update) | async-done | bytes 1441808 | tf_op jit(solution)/shard_map/psum | solution.py:57
  614.4 2.6 fusion.71
  617.0 23.1 %all_to_all.5 = bf16[32,8,1024]{2,1,0:T(8,128)(2,1)S(1)} all-to-all(bf16[32,8,1024]{2,1,0:T(8,128)(2,1)S(1)} %fusion.71), channel_id=1, replica_groups=mesh['tm'=32,'tensor'=4] {'tm'}, dimensions={0} | all-to-all | bytes 1048576 | tf_op jit(solution)/shard_map/all_to_all | solution.py:134
  (69 shorter events, 32.9 us)
Async XLA Ops:
  6.5 89.1 %all-gather.9.cloned.1.call-start = ((), (), s32[]{:S(2)}) async-start(), calls=%async_computation.1 | async-start | bytes 4460544 | tf_op jit(solution)/shard_map/all_gather | solution.py:67
  8.2 307.8 %all-reduce.3.cloned.1.call-start = ((), (), s32[]{:S(2)}) async-start(), calls=%async_computation.2 | async-start | bytes 2883584 | tf_op jit(solution)/shard_map/psum | solution.py:57
  12.5 90.8 %copy-start = (bf16[512,1408]{1,0:T(8,128)(2,1)S(1)}, bf16[512,1408]{1,0:T(8,128)(2,1)}, u32[]{:S(2)}) copy-start(bf16[512,1408]{1,0:T(8,128)(2,1)} %param.11) | copy-start | bytes 4325380
  12.5 90.8 %copy-start.8 = (f32[1408]{0:T(1024)S(1)}, f32[1408]{0:T(1024)}, u32[]{:S(2)}) copy-start(f32[1408]{0:T(1024)} %param.12) | copy-start | bytes 16900
  103.3 9.7 %copy-start.5 = (bf16[352,44]{0,1:T(8,128)(2,1)S(1)}, bf16[352,44]{0,1:T(8,128)(2,1)}, u32[]{:S(2)}) copy-start(bf16[352,44]{0,1:T(8,128)(2,1)} %param.14) | copy-start | bytes 92932
  107.2 1.0 copy-start.4
  108.4 112.3 %collective-permute-start = (bf16[256,2,352]{2,0,1:T(8,128)(2,1)S(1)}, bf16[256,2,352]{2,0,1:T(8,128)(2,1)S(1)}, u32[]{:S(2)}, u32[]{:S(2)}) collective-permute-start(bf16[256,2,352]{2,0,1:T(8,128)(2,1)S(1)} %copy.35), channel_id=1, source_target_pairs={{0,4},{4,8},{8,12},{12,16},{16,20},{20,24},{24,28},{28,32},{32,36}... | collective-permute-start | bytes 1081352 | tf_op jit(solution)/shard_map/ppermute | solution.py:24
  111.7 109.1 %collective-permute-start.1 = (bf16[256,2,352]{2,0,1:T(8,128)(2,1)}, bf16[256,2,352]{2,0,1:T(8,128)(2,1)}, u32[]{:S(2)}, u32[]{:S(2)}) collective-permute-start(bf16[256,2,352]{2,0,1:T(8,128)(2,1)} %copy.37), channel_id=1, source_target_pairs={{4,0},{8,4},{12,8},{16,12},{20,16},{24,20},{28,24},{32,28},{36,32}... | collective-permute-start | bytes 1081352 | tf_op jit(solution)/shard_map/ppermute | solution.py:27
  247.4 6.2 copy-start.2
  265.1 5.2 copy-start.3
  272.4 132.3 %all-gather.11.cloned.1.call-start = ((), (), s32[]{:S(2)}) async-start(), calls=%async_computation.4 | async-start | bytes 4866048 | tf_op jit(solution)/shard_map/all_gather | solution.py:69
  273.1 215.8 %all-gather.13.cloned.1.call-start = ((), (), s32[]{:S(2)}) async-start(), calls=%async_computation.5 | async-start | bytes 4866048 | tf_op jit(solution)/shard_map/all_gather | solution.py:70
  273.7 291.9 %all-gather.15.cloned.1.call-start = ((), (), s32[]{:S(2)}) async-start(), calls=%async_computation.6 | async-start | bytes 3244032 | tf_op jit(solution)/shard_map/all_gather | solution.py:71
  274.3 337.2 %all-reduce.5.cloned.1.call-start = ((), (), s32[]{:S(2)}) async-start(), calls=%async_computation.3 | async-start | bytes 2883584 | tf_op jit(solution)/shard_map/psum | solution.py:57
  315.9 1.9 copy-start.1
  411.7 84.3 %copy-start.9 = (f32[1408]{0:T(1024)S(1)}, f32[1408]{0:T(1024)}, u32[]{:S(2)}) copy-start(f32[1408]{0:T(1024)} %param.15) | copy-start | bytes 16900
  496.0 15.1 %copy-start.7 = (s32[512]{0:T(512)S(1)}, s32[512]{0:T(512)}, u32[]{:S(2)}) copy-start(s32[512]{0:T(512)} %param.20) | copy-start | bytes 6148
  496.0 15.2 %copy-start.6 = (s32[128,1]{0,1:T(1,128)S(1)}, s32[128,1]{0,1:T(1,128)}, u32[]{:S(2)}) copy-start(s32[128,1]{0,1:T(1,128)} %param.21) | copy-start | bytes 1540
Sparse Core Ops, SparseCore 0:
  10.3 85.2 all-gather.8
  272.5 43.4 all-reduce.2
  318.9 85.6 all-gather.10
  407.4 81.4 all-gather.12
  491.7 73.8 all-gather.14
  568.0 43.4 all-reduce.4
where the time goes:
time: 649 us; the launch traced here: 648 us
  waiting for transfers between devices  384 us (59%)
  blocking collectives  125 us (19%)
  local copies, waits for them, and re-layouts  75.8 us (12%)
  matrix products  31.7 us (5%)
  between operations  13.7 us (2%)
  other arithmetic  13.3 us (2%)
    all_gather x1, blocking collectives, body(): lax.all_gather(w_out, 'tm', axis=1, tiled=True)  102 us
    all_gather x1, waiting for transfers between devices, body(): lax.all_gather(w_up, 'tm', axis=0, tiled=True)  86.1 us
    all_gather x1, waiting for transfers between devices, body(): lax.all_gather(w_qkv, 'tm', axis=0, tiled=True)  83.1 us
    psum x2, waiting for transfers between devices, tensor_total(): return lax.psum(term.astype(jnp.bfloat16), 'tensor').astype(jnp.float32)  82 us
    all_gather x1, waiting for transfers between devices, body(): lax.all_gather(w_down, 'tm', axis=1, tiled=True)  77.3 us
    all_gather x1, waiting for transfers between devices, body(): lax.all_gather(w_proj, 'tm', axis=0, tiled=True)  54 us
    unnamed x31, local copies, waits for them, and re-layouts  38.5 us
    all_to_all x1, blocking collectives, body(): lax.all_to_all(outbox, 'tm', split_axis=0, concat_axis=0, tiled=True)  23.1 us
  transfers between devices with their start and end apart: 8, of which 6 were waited for; matrix products, arithmetic and copies ran while one was open for 7% of the time, Pallas kernels for 0%

commit v1 on v0

--- a/solution.py
+++ b/solution.py
@@ -1,8 +1,11 @@
+import functools
 import math
 
 import jax
 import jax.numpy as jnp
 from jax import lax
+from jax.experimental import pallas as pl
+from jax.experimental.pallas import tpu as pltpu
 from jax.sharding import PartitionSpec as P
 
 D = 1408
@@ -11,9 +14,171 @@
 BLK = 64
 WIN = 8
 POOL = 4
-
+N_TM = 32
+ROWS = D // N_TM
+PROWS = 48
+DP = N_TM * PROWS
 
 eps = 1e-06
+MESH = pl.DeviceIdType.MESH
+OFFSETS = (0, -1, 1, 2)
+N_EVENTS = 20
+
+
+class RingGather:
+    def __init__(self, own, bufs, send_sems, recv_sems, local_sems, z_sems):
+        self.own, self.bufs = own, bufs
+        self.send_sems, self.recv_sems = send_sems, recv_sems
+        self.local_sems, self.z_sems = local_sems, z_sems
+        self.tm = lax.axis_index("tm")
+        self.t = lax.axis_index("tensor")
+        self.x = self.tm // 8
+        self.y = (self.tm // 2) % 4
+        self.zh = self.tm % 2
+
+    def colour(self, fam):
+        return self.zh if fam == 0 else 1 - self.zh
+
+    def at(self, fam, a, b, z):
+        k = self.colour(fam)
+        dx = a * (1 - k) + b * k
+        dy = a * k + b * (1 - k)
+        return (((self.x + dx + 4) % 4) * 4 + (self.y + dy + 4) % 4) * 2 + z
+
+    def device(self, fam, a, b):
+        return (self.at(fam, a, b, self.zh), self.t)
+
+    def part(self, c, fam, a, b, half):
+        buf = self.bufs[c]
+        slot = self.at(fam, a, b, self.colour(fam))
+        if half is None:
+            return buf.at[slot]
+        n = buf.shape[2]
+        cut = (n // 2 + 127) // 128 * 128
+        return buf.at[slot, :, pl.ds(0, cut) if half == 0 else pl.ds(cut, n - cut)]
+
+    def event(self, c, fam, ev):
+        if ev < 4:
+            a, b, half, da, db = ((0, 0, None, 1, 0), (0, 0, None, -1, 0), (-1, 0, 0, 1, 0), (1, 0, 1, -1, 0))[ev]
+        else:
+            off = OFFSETS[(ev - 4) // 4]
+            a, b, half, da, db = (
+                (off, 0, None, 0, 1), (off, 0, None, 0, -1), (off, -1, 0, 0, 1), (off, 1, 1, 0, -1)
+            )[(ev - 4) % 4]
+        src = self.part(c, fam, a, b, half)
+        if fam == 0 and a == 0 and b == 0:
+            src = self.own[c]
+        dst = self.part(c, fam, a, b, half)
+        landed = self.part(c, fam, a - da if a - da > -2 else 2, b - db if b - db > -2 else 2, half)
+        sem = (c * 2 + fam) * N_EVENTS + ev
+        return src, dst, landed, sem, self.device(fam, da, db)
+
+    def start(self, c, fam, *events):
+        for ev in events:
+            src, dst, _, sem, dev = self.event(c, fam, ev)
+            pltpu.make_async_remote_copy(
+                src_ref=src, dst_ref=dst, send_sem=self.send_sems.at[sem], recv_sem=self.recv_sems.at[sem],
+                device_id=dev, device_id_type=MESH,
+            ).start()
+
+    def wait(self, c, fam, *events):
+        for ev in events:
+            _, _, landed, sem, dev = self.event(c, fam, ev)
+            pltpu.make_async_remote_copy(
+                src_ref=landed, dst_ref=landed, send_sem=self.send_sems.at[sem], recv_sem=self.recv_sems.at[sem],
+                device_id=dev, device_id_type=MESH,
+            ).wait_recv()
+
+    def wait_sends(self):
+        for c in range(len(self.own)):
+            for fam in range(2):
+                for ev in range(N_EVENTS):
+                    src, dst, _, sem, dev = self.event(c, fam, ev)
+                    pltpu.make_async_remote_copy(
+                        src_ref=src, dst_ref=dst, send_sem=self.send_sems.at[sem], recv_sem=self.recv_sems.at[sem],
+                        device_id=dev, device_id_type=MESH,
+                    ).wait_send()
+            self.z_copy(c, self.tm).wait_send()
+
+    def z_copy(self, c, slot):
+        partner = self.tm + 1 - 2 * self.zh
+        return pltpu.make_async_remote_copy(
+            src_ref=self.own[c], dst_ref=self.bufs[c].at[slot],
+            send_sem=self.z_sems.at[0, c], recv_sem=self.z_sems.at[1, c],
+            device_id=(partner, self.t), device_id_type=MESH,
+        )
+
+    def local(self, c):
+        return pltpu.make_async_copy(self.own[c], self.bufs[c].at[self.tm], self.local_sems.at[c])
+
+    def barrier(self):
+        sem = pltpu.get_barrier_semaphore()
+        devs = [self.device(0, 1, 0), self.device(0, -1, 0), self.device(0, 0, 1), self.device(0, 0, -1),
+                (self.tm + 1 - 2 * self.zh, self.t)]
+        for dev in devs:
+            pl.semaphore_signal(sem, inc=1, device_id=dev, device_id_type=MESH)
+        pl.semaphore_wait(sem, len(devs))
+
+    def stage(self, c, s):
+        if s == 0:
+            self.z_copy(c, self.tm).start()
+            self.start(c, 0, 0, 1, 4, 5)
+            self.local(c).start()
+        elif s == 1:
+            self.z_copy(c, self.tm + 1 - 2 * self.zh).wait_recv()
+            self.start(c, 1, 0, 1, 4, 5)
+            self.local(c).wait()
+        elif s < 6:
+            for fam in range(2):
+                if s == 2:
+                    self.wait(c, fam, 0)
+                    self.start(c, fam, 2, 8, 9)
+                    self.wait(c, fam, 1)
+                    self.start(c, fam, 3, 12, 13)
+                    for ev in (4, 5):
+                        self.wait(c, fam, ev)
+                        self.start(c, fam, ev + 2)
+                elif s == 3:
+                    self.wait(c, fam, 2, 3)
+                    self.start(c, fam, 16, 17)
+                    for ev in (8, 9, 12, 13):
+                        self.wait(c, fam, ev)
+                        self.start(c, fam, ev + 2)
+                elif s == 4:
+                    for ev in (16, 17):
+                        self.wait(c, fam, ev)
+                        self.start(c, fam, ev + 2)
+                else:
+                    self.wait(c, fam, 6, 7, 10, 11, 14, 15, 18, 19)
+
+
+def gather_kernel(n, *refs):
+    own, bufs, sems = refs[:n], refs[n:2 * n], refs[2 * n:]
+    g = RingGather(own, bufs, *sems)
+    g.barrier()
+    for tick in range(n + 5):
+        for c in range(n):
+            if 0 <= tick - c < 6:
+                g.stage(c, tick - c)
+    g.wait_sends()
+
+
+def gather_weights(parts):
+    n = len(parts)
+    vmem = pl.BlockSpec(memory_space=pltpu.VMEM)
+    return pl.pallas_call(
+        functools.partial(gather_kernel, n),
+        out_shape=[jax.ShapeDtypeStruct((N_TM, PROWS, p.shape[1]), jnp.bfloat16) for p in parts],
+        in_specs=[vmem] * n,
+        out_specs=[vmem] * n,
+        scratch_shapes=[
+            pltpu.SemaphoreType.DMA((n * 2 * N_EVENTS,)),
+            pltpu.SemaphoreType.DMA((n * 2 * N_EVENTS,)),
+            pltpu.SemaphoreType.DMA((n,)),
+            pltpu.SemaphoreType.DMA((2, n)),
+        ],
+        compiler_params=pltpu.CompilerParams(collective_id=0, has_side_effects=True, vmem_limit_bytes=60 << 20),
+    )(*parts)
 
 
 def with_halo(block, sides, width):
@@ -29,10 +194,21 @@
     return block
 
 
+def pad_features(values):
+    src = jnp.arange(D, dtype=jnp.int32)
+    place = (src // ROWS * PROWS + src % ROWS)[:, None] == jnp.arange(DP, dtype=jnp.int32)[None, :]
+    return jnp.dot(values, place.astype(values.dtype), preferred_element_type=jnp.float32)
+
+
+def pad_gain(gain):
+    return jnp.pad(gain.reshape(N_TM, ROWS), ((0, 0), (0, PROWS - ROWS))).reshape(1, DP)
+
+
 def layer_norm(values, scales):
-    average = jnp.mean(values, axis=-1, keepdims=True)
-    centred = values - average
-    spread = jnp.mean(centred * centred, axis=-1, keepdims=True)
+    real = (jnp.arange(DP, dtype=jnp.int32) % PROWS < ROWS).astype(jnp.float32)[None, :]
+    average = jnp.sum(values, axis=-1, keepdims=True) * (1.0 / D)
+    centred = (values - average) * real
+    spread = jnp.sum(centred * centred, axis=-1, keepdims=True) * (1.0 / D)
     return (centred * lax.rsqrt(spread + eps) * scales).astype(jnp.bfloat16)
 
 
@@ -57,25 +233,28 @@
     return lax.psum(term.astype(jnp.bfloat16), "tensor").astype(jnp.float32)
 
 
+def nt_dot(a, b):
+    return lax.dot_general(a, b, (((1,), (1,)), ((), ())), preferred_element_type=jnp.float32)
+
+
 def body(
     frames, gain_attn, w_qkv, w_out, gain_mlp, w_up, w_down, w_proj, windows, pool_map, owners
 ):
     row_count = frames.shape[0]
     query_blocks = row_count // BLK
     head_dim = D // HEADS
-    full_qkv, full_out, full_up, full_down, full_proj = (
-        lax.all_gather(w_qkv, "tm", axis=0, tiled=True),
-        lax.all_gather(w_out, "tm", axis=1, tiled=True),
-        lax.all_gather(w_up, "tm", axis=0, tiled=True),
-        lax.all_gather(w_down, "tm", axis=1, tiled=True),
-        lax.all_gather(w_proj, "tm", axis=0, tiled=True),
-    )
-    local_width = full_qkv.shape[2]
+    local_width = w_qkv.shape[2]
+    pad = lambda w: jnp.pad(w, ((0, PROWS - ROWS), (0, 0)))
+    parts = [
+        pad(w_qkv.reshape(ROWS, 3 * local_width)), pad(w_out.T), pad(w_up), pad(w_down.T), pad(w_proj)
+    ]
+    full_qkv, full_out_t, full_up, full_down_t, full_proj = [
+        w.reshape(DP, w.shape[2]) for w in gather_weights(parts)
+    ]
     heads_here = local_width // head_dim
-    normed = layer_norm(frames.astype(jnp.float32), gain_attn)
-    projected_qkv = jnp.dot(
-        normed, full_qkv.reshape(D, 3 * local_width), preferred_element_type=jnp.float32
-    ).astype(jnp.bfloat16)
+    frames_wide = pad_features(frames)
+    normed = layer_norm(frames_wide, pad_gain(gain_attn))
+    projected_qkv = jnp.dot(normed, full_qkv, preferred_element_type=jnp.float32).astype(jnp.bfloat16)
     projected_qkv = projected_qkv.reshape(row_count, 3, local_width)
     keyvals = with_halo(projected_qkv[:, 1:, :], (("tm", 0),), PATCHES)
     per_frame = PATCHES // BLK
@@ -106,15 +285,13 @@
     attended = lax.map(
         attend_group, (queries, local_ids.reshape(query_blocks // group_size, group_size, WIN))
     ).reshape(row_count, local_width)
-    mixed_term = jnp.dot(attended, full_out, preferred_element_type=jnp.float32)
-    stream = frames.astype(jnp.float32) + tensor_total(mixed_term)
-    hidden = layer_norm(stream, gain_mlp)
+    mixed_term = nt_dot(attended, full_out_t)
+    stream = frames_wide + tensor_total(mixed_term)
+    hidden = layer_norm(stream, pad_gain(gain_mlp))
     activation = jax.nn.gelu(
         jnp.dot(hidden, full_up, preferred_element_type=jnp.float32), approximate=False
     ).astype(jnp.bfloat16)
-    stream = stream + tensor_total(
-        jnp.dot(activation, full_down, preferred_element_type=jnp.float32)
-    )
+    stream = stream + tensor_total(nt_dot(activation, full_down_t))
     pooled = pool_rows(stream, pool_map)
     proj_rows = jnp.dot(pooled, full_proj, preferred_element_type=jnp.float32).astype(jnp.bfloat16)
     pooled_count = proj_rows.shape[0]

time: 649 us -> 368 us (0.57)
  waiting for transfers between devices: 384 us -> 108 us
  Pallas kernels: 0 us -> 111 us
  blocking collectives: 125 us -> 23.1 us
  local copies, waits for them, and re-layouts: 75.8 us -> 51.8 us
    all_gather x4 -> x0, waiting for transfers between devices: 300 us -> none  [the longest x1 86.1 us: body(): lax.all_gather(w_up, 'tm', axis=0, tiled=True)]
    pallas_call x0 -> x1, Pallas kernels: none -> 111 us  [gather_weights(): pl.pallas_call(functools.partial(gather_kernel, n), out_shape=[jax.ShapeD...]
    all_gather x1 -> x0, blocking collectives: 102 us -> none  [body(): lax.all_gather(w_out, 'tm', axis=1, tiled=True)]
    unnamed x31 -> x27, local copies, waits for them, and re-layouts: 38.5 us -> 17.2 us
    psum x2, waiting for transfers between devices: 82 us -> 99.5 us  [tensor_total(): return lax.psum(term.astype(jnp.bfloat16), 'tensor').astype(jnp.float32)]
    all_gather x1 -> x0, local copies, waits for them, and re-layouts: 7.69 us -> none  [body(): lax.all_gather(w_qkv, 'tm', axis=0, tiled=True)]
    ppermute x1, waiting for transfers between devices: 0.01 us -> 7.1 us  [with_halo(): lax.ppermute(lax.slice_in_dim(block, block.shape[dim] - width, None, axis...]
    pad x0 -> x7, local copies, waits for them, and re-layouts: none -> 6.74 us  [the longest x5 6.73 us: body(): pad = lambda w: jnp.pad(w, ((0, PROWS - ROWS), (0, 0)))]
  transfers between devices with their start and end apart: 8 -> 4, of which waited for: 6 -> 4; matrix products, arithmetic and copies ran while one was open for 7% -> 1% of each run, Pallas kernels for 0% -> 0%
where the time goes in v1:
time: 368 us; the launch traced here: 367 us
  Pallas kernels  111 us (30%)
  waiting for transfers between devices  108 us (29%)
  local copies, waits for them, and re-layouts  51.8 us (14%)
  matrix products  34.1 us (9%)
  blocking collectives  23.1 us (6%)
  other arithmetic  16.8 us (5%)
  between operations  13.7 us (4%)
  starting transfers between devices  8.36 us (2%)
    pallas_call x1, Pallas kernels, gather_weights(): pl.pallas_call(functools.partial(gather_kernel, n), out_shape=[jax.ShapeD...  111 us
    psum x2, waiting for transfers between devices, tensor_total(): return lax.psum(term.astype(jnp.bfloat16), 'tensor').astype(jnp.float32)  99.5 us
    all_to_all x1, blocking collectives, body(): lax.all_to_all(outbox, 'tm', split_axis=0, concat_axis=0, tiled=True)  23.1 us
    dot_general x2, matrix products, nt_dot(): lax.dot_general(a, b, (((1,), (1,)), ((), ())), preferred_element_type=jn...  18.4 us
    unnamed x27, local copies, waits for them, and re-layouts  17.2 us
    gather x2, local copies, waits for them, and re-layouts, attend_group(): kv_blocks[id_group].reshape(group_size, WIN * BLK, 2, heads_here, head_dim)  14.9 us
  transfers between devices with their start and end apart: 4, of which 4 were waited for; matrix products, arithmetic and copies ran while one was open for 1% of the time, Pallas kernels for 0%

profile of v1, /device:TPU:0, one launch (start us, length us, event | category | flops | bytes accessed | tf_op | source)
XLA Modules:
  0.0 367.0 jit_solution(3621000255903563480)
XLA Ops:
  15.4 3.0 fusion.126
  18.4 1.6 copy-done.2
  20.6 111.3 %shard_map.109 = (bf16[32,48,1056]{2,1,0:T(8,128)(2,1)}, bf16[32,48,352]{2,1,0:T(8,128)(2,1)}, bf16[32,48,1536]{2,1,0:T(8,128)(2,1)}, bf16[32,48,1536]{2,1,0:T(8,128)(2,1)}, bf16[32,48,1024]{2,1,0:T(8,128)(2,1)}) custom-call(bf16[48,1056]{1,0:T(8,128)(2,1)} %pad.27.refs_0_, bf16[48,352]{1,0:T(8,128)(2,1)} %pad.28.refs_1_, bf16[48,1536]{1,0:T(8,128)(2,1)} %pad.29.refs_2_, ...), custom_call_target="tpu_custom_call" | custom-call | tf_op jit(solution)/shard_map/pallas_call | solution.py:169
  131.9 5.1 %convolution_convert_fusion = bf16[512,1056]{0,1:T(8,128)(2,1)S(1)} fusion(bf16[1536,1056]{1,0:T(8,128)(2,1)} %bitcast.76, f32[1536,512]{0,1:T(8,128)} %copy-done.2, f32[1536]{0:T(1024)S(1)} %mul.153, f32[512]{0:T(512)S(1)} %add_rsqrt_fusion.1, f32[1536]{0:T(1024)S(1)} %fusion.92, f32[512]{0:T(512)S(1)} %broadcast_multiply_fusion.1), kind=kOutput, calls=%fused_computation.37 | convolution fusion | flops 1665417216 | bytes 7487488 | tf_op jit(solution)/shard_map/dot_general | solution.py:257
  138.8 6.8 %collective-permute-start = (bf16[256,2,352]{2,0,1:T(8,128)(2,1)S(1)}, bf16[256,2,352]{2,0,1:T(8,128)(2,1)}, u32[]{:S(2)}, u32[]{:S(2)}) collective-permute-start(bf16[256,2,352]{2,0,1:T(8,128)(2,1)S(1)} %copy.24), channel_id=1, source_target_pairs={{0,4},{4,8},{8,12},{12,16},{16,20},{20,24},{24,28},{28,32},{32,36}... | collective-permute-start | bytes 1081352 | tf_op jit(solution)/shard_map/ppermute | solution.py:189
  148.5 7.1 %collective-permute-done = bf16[256,2,352]{2,0,1:T(8,128)(2,1)} collective-permute-done((bf16[256,2,352]{2,0,1:T(8,128)(2,1)S(1)}, bf16[256,2,352]{2,0,1:T(8,128)(2,1)}, u32[]{:S(2)}, u32[]{:S(2)}) %collective-permute-start) | collective-permute-done | bytes 360480 | tf_op jit(solution)/shard_map/ppermute | solution.py:189
  157.0 2.3 reshape.127
  159.3 2.1 copy.17
  161.4 5.5 %gather_fusion = bf16[64,64,2,4,88]{4,1,3,2,0:T(8,128)(2,1)} fusion(bf16[16,64,2,4,88]{4,1,3,2,0:T(8,128)(2,1)S(1)} %copy.17, s32[1024]{0:T(1024)S(1)} %pad_clamp_fusion), kind=kCustom, calls=%fused_computation | custom fusion | bytes 11534592 | tf_op jit(solution)/shard_map/while/body/eval_jaxpr/gather | solution.py:271
  166.9 9.4 %copy.18 = bf16[64,64,2,4,88]{4,1,0,3,2:T(8,128)(2,1)} copy(bf16[64,64,2,4,88]{4,1,3,2,0:T(8,128)(2,1)} %gather_fusion) | data formatting | bytes 11534336 | tf_op jit(solution)/shard_map/while/body/eval_jaxpr/gather | solution.py:271
  176.3 5.9 %fusion.124 = (bf16[8,512,1,4,88]{4,1,0,3,2:T(8,128)(2,1)}, bf16[8,512,1,4,88]{4,1,0,3,2:T(8,128)(2,1)}) fusion(bf16[8,512,2,4,88]{4,1,0,3,2:T(8,128)(2,1)} %bitcast.61), kind=kLoop, calls=%fused_computation.159 | loop fusion | bytes 11534336 | tf_op jit(solution)/shard_map/while/body/eval_jaxpr/slice | solution.py:282
  182.2 6.1 %copy.27 = bf16[8,512,1,4,88]{1,4,3,0,2:T(8,128)(2,1)} copy(bf16[8,512,1,4,88]{4,1,0,3,2:T(8,128)(2,1)} %get-tuple-element.30) | data formatting | bytes 5767168
  188.3 6.1 %copy.29 = bf16[8,512,1,4,88]{1,4,3,0,2:T(8,128)(2,1)} copy(bf16[8,512,1,4,88]{4,1,0,3,2:T(8,128)(2,1)} %get-tuple-element.31) | data formatting | bytes 5767168
  194.4 2.6 fusion.17
  197.0 6.0 %fusion.127 = (f32[8,4,64]{2,1,0:T(4,128)S(1)}, f32[8,4,64,512]{3,2,1,0:T(8,128)S(1)}) fusion(f32[8,4,64,512]{3,2,1,0:T(8,128)S(1)} %fusion.17), kind=kOutput, calls=%fused_computation.162 | output fusion | flops 4194815 | bytes 8396800 | tf_op jit(solution)/shard_map/while/body/eval_jaxpr/sub | solution.py:279
  205.1 2.2 convolution_convert_fusion.2
  207.7 50.0 %all-reduce.10.cloned.1.call-done = bf16[512,1536]{1,0:T(8,128)(2,1)} async-done(((bf16[512,1536]{1,0:T(8,128)(2,1)}), bf16[512,1536]{1,0:T(8,128)(2,1)}) %all-reduce.10.cloned.1.call-update) | async-done | bytes 1572880 | tf_op jit(solution)/shard_map/psum | solution.py:233
  257.7 2.9 fusion.75
  260.6 2.6 multiply_reduce_fusion.1
  263.3 16.2 %convolution_convert_fusion.1 = bf16[512,1536]{1,0:T(8,128)(2,1)} fusion(bf16[1536,1536]{1,0:T(8,128)(2,1)} %bitcast.75, bf16[1536,1536]{1,0:T(8,128)(2,1)} %bitcast.74, f32[1536]{0:T(1024)S(1)} %mul.164, f32[512]{0:T(512)S(1)} %add_rsqrt_fusion, f32[512]{0:T(512)S(1)} %broadcast_multiply_fusion, f32[1536]{0:T(1024)S(1)} %fusion.92, ...), kind=kOutput, calls=%fused_computation.38 | convolution fusion | flops 4889247744 | bytes 15745024 | tf_op jit(solution)/shard_map/dot_general | solution.py:237
  280.0 49.4 %all-reduce.12.cloned.1.call-done = bf16[512,1536]{1,0:T(8,128)(2,1)} async-done(((bf16[512,1536]{1,0:T(8,128)(2,1)}), bf16[512,1536]{1,0:T(8,128)(2,1)}) %all-reduce.12.cloned.1.call-update) | async-done | bytes 1572880 | tf_op jit(solution)/shard_map/psum | solution.py:233
  329.5 3.0 convert_add_fusion
  333.6 2.7 fusion.70
  336.3 23.1 %all_to_all.5 = bf16[32,8,1024]{2,1,0:T(8,128)(2,1)S(1)} all-to-all(bf16[32,8,1024]{2,1,0:T(8,128)(2,1)S(1)} %fusion.70), channel_id=1, replica_groups=mesh['tm'=32,'tensor'=4] {'tm'}, dimensions={0} | all-to-all | bytes 1048576 | tf_op jit(solution)/shard_map/all_to_all | solution.py:311
  (66 shorter events, 20.4 us)
Async XLA Ops:
  6.5 8.9 %copy-start = (bf16[512,1408]{1,0:T(8,128)(2,1)S(1)}, bf16[512,1408]{1,0:T(8,128)(2,1)}, u32[]{:S(2)}) copy-start(bf16[512,1408]{1,0:T(8,128)(2,1)} %param.11) | copy-start | bytes 4325380
  6.5 251.2 %all-reduce.10.cloned.1.call-start = ((), (), s32[]{:S(2)}) async-start(), calls=%async_computation.1 | async-start | bytes 3145728 | tf_op jit(solution)/shard_map/psum | solution.py:233
  18.4 1.6 copy-start.2
  137.0 8.7 %copy-start.7 = (s32[8,8]{1,0:T(8,128)S(1)}, s32[8,8]{1,0:T(8,128)}, u32[]{:S(2)}) copy-start(s32[8,8]{1,0:T(8,128)} %param.19) | copy-start | bytes 772
  137.3 11.2 %collective-permute-start.1 = (bf16[256,2,352]{2,0,1:T(8,128)(2,1)S(1)}, bf16[256,2,352]{2,0,1:T(8,128)(2,1)S(1)}, u32[]{:S(2)}, u32[]{:S(2)}) collective-permute-start(bf16[256,2,352]{2,0,1:T(8,128)(2,1)S(1)} %copy.26), channel_id=1, source_target_pairs={{4,0},{8,4},{12,8},{16,12},{20,16},{24,20},{28,24},{32,28},{36,32}... | collective-permute-start | bytes 1081352 | tf_op jit(solution)/shard_map/ppermute | solution.py:192
  138.8 16.8 %collective-permute-start = (bf16[256,2,352]{2,0,1:T(8,128)(2,1)S(1)}, bf16[256,2,352]{2,0,1:T(8,128)(2,1)}, u32[]{:S(2)}, u32[]{:S(2)}) collective-permute-start(bf16[256,2,352]{2,0,1:T(8,128)(2,1)S(1)} %copy.24), channel_id=1, source_target_pairs={{0,4},{4,8},{8,12},{12,16},{16,20},{20,24},{24,28},{28,32},{32,36}... | collective-permute-start | bytes 1081352 | tf_op jit(solution)/shard_map/ppermute | solution.py:189
  197.0 6.0 %copy-start.4 = (bf16[8,512,1,4,88]{1,4,3,0,2:T(8,128)(2,1)S(1)}, bf16[8,512,1,4,88]{1,4,3,0,2:T(8,128)(2,1)}, u32[]{:S(2)}) copy-start(bf16[8,512,1,4,88]{1,4,3,0,2:T(8,128)(2,1)} %copy.27) | copy-start | bytes 8650756
  203.0 2.1 copy-start.5
  204.3 3.3 copy-start.6
  207.2 122.2 %all-reduce.12.cloned.1.call-start = ((), (), s32[]{:S(2)}) async-start(), calls=%async_computation.2 | async-start | bytes 3145728 | tf_op jit(solution)/shard_map/psum | solution.py:233
  257.7 2.9 copy-start.3
  263.2 16.2 %copy-start.9 = (s32[512]{0:T(512)S(1)}, s32[512]{0:T(512)}, u32[]{:S(2)}) copy-start(s32[512]{0:T(512)} %param.20) | copy-start | bytes 6148
  263.3 16.3 %copy-start.8 = (s32[128,1]{0,1:T(1,128)S(1)}, s32[128,1]{0,1:T(1,128)}, u32[]{:S(2)}) copy-start(s32[128,1]{0,1:T(1,128)} %param.21) | copy-start | bytes 1540
  332.4 27.8 %copy-start.1 = (bf16[512,1408]{1,0:T(8,128)(2,1)S(1)}, bf16[512,1408]{1,0:T(8,128)(2,1)}, u32[]{:S(2)}) copy-start(bf16[512,1408]{1,0:T(8,128)(2,1)} %param.11) | copy-start | bytes 4325380
Sparse Core Ops, SparseCore 0:
  207.4 50.3 all-reduce.9
  279.6 49.8 all-reduce.11

commit v2 on v0

v2 whole, which is shorter than its diff:
```python
import functools

import jax
import jax.numpy as jnp
from jax import lax
from jax.experimental import pallas as pl
from jax.experimental.pallas import tpu as pltpu
from jax.sharding import PartitionSpec as P

D = 1408
HEADS = 16
PATCHES = 256
BLK = 64
WIN = 8
POOL = 4
N_TM = 32
HEAD_DIM = D // HEADS
HERE = 4
HW = 384
ROWS = D // N_TM
PROWS = 48
DP = N_TM * PROWS
FF8 = 768
LM8 = 512
WIDTHS = (3 * HW, HW, FF8, FF8, LM8)
QKV, OUT, UP, DOWN, PROJ = range(5)
START = (0, 2, 4, 6, 8)

eps = 1e-06
MESH = pl.DeviceIdType.MESH
OFFSETS = (0, -1, 1, 2)
N_EVENTS = 20
F32 = jnp.float32
BF16 = jnp.bfloat16


class Place:
    def __init__(self):
        self.tm = lax.axis_index("tm")
        self.t = lax.axis_index("tensor")
        self.xy = self.tm // 2
        self.x = self.tm // 8
        self.y = self.xy % 4
        self.zh = self.tm % 2
        self.zl = self.t // 2
        self.c = self.t % 2
        self.z = self.zh * 2 + self.zl
        self.partner = self.tm + 1 - 2 * self.zh

    def ring(self, dz, c):
        z = (self.z + dz + 4) % 4
        return (self.xy * 2 + z // 2, (z % 2) * 2 + c)


class Copies:
    def __init__(self, send_sems, recv_sems):
        self.send_sems, self.recv_sems = send_sems, recv_sems
        self.used = 0
        self.sent = []

    def take(self, n=1):
        self.used += n
        return self.used - n

    def make(self, src, dst, sem, dev):
        return pltpu.make_async_remote_copy(
            src_ref=src, dst_ref=dst, send_sem=self.send_sems.at[sem], recv_sem=self.recv_sems.at[sem],
            device_id=dev, device_id_type=MESH,
        )

    def start(self, src, dst, sem, dev):
        copy = self.make(src, dst, sem, dev)
        copy.start()
        self.sent.append(copy)

    def arrived(self, landed, sem, dev):
        self.make(landed, landed, sem, dev).wait_recv()

    def drain(self):
        for copy in self.sent:
            copy.wait_send()
        self.sent = []


class RingGather:
    def __init__(self, place, copies, parts, bufs, local_sems):
        self.p, self.copies, self.parts, self.bufs, self.local_sems = place, copies, parts, bufs, local_sems
        self.base = [copies.take(2 * N_EVENTS + 1) for _ in parts]

    def own(self, c):
        return self.parts[c] if c < UP else self.parts[c].at[self.p.zh]

    def theirs(self, c):
        return self.parts[c] if c < UP else self.parts[c].at[1 - self.p.zh]

    def colour(self, fam):
        return self.p.zh if fam == 0 else 1 - self.p.zh

    def at(self, fam, a, b, z):
        k = self.colour(fam)
        dx = a * (1 - k) + b * k
        dy = a * k + b * (1 - k)
        return (((self.p.x + dx + 4) % 4) * 4 + (self.p.y + dy + 4) % 4) * 2 + z

    def part(self, c, fam, a, b, half):
        buf = self.bufs[c]
        slot = self.at(fam, a, b, self.colour(fam))
        if half is None:
            return buf.at[slot]
        n = buf.shape[2]
        cut = (n // 2 + 127) // 128 * 128
        return buf.at[slot, :, pl.ds(0, cut) if half == 0 else pl.ds(cut, n - cut)]

    def event(self, c, fam, ev):
        if ev < 4:
            a, b, half, da, db = ((0, 0, None, 1, 0), (0, 0, None, -1, 0), (-1, 0, 0, 1, 0), (1, 0, 1, -1, 0))[ev]
        else:
            off = OFFSETS[(ev - 4) // 4]
            a, b, half, da, db = (
                (off, 0, None, 0, 1), (off, 0, None, 0, -1), (off, -1, 0, 0, 1), (off, 1, 1, 0, -1)
            )[(ev - 4) % 4]
        dst = self.part(c, fam, a, b, half)
        src = self.own(c) if fam == 0 and a == 0 and b == 0 else dst
        landed = self.part(c, fam, a - da if a - da > -2 else 2, b - db if b - db > -2 else 2, half)
        sem = self.base[c] + fam * N_EVENTS + ev
        return src, dst, landed, sem, (self.at(fam, da, db, self.p.zh), self.p.t)

    def start(self, c, fam, *events):
        for ev in events:
            src, dst, _, sem, dev = self.event(c, fam, ev)
            self.copies.start(src, dst, sem, dev)

    def wait(self, c, fam, *events):
        for ev in events:
            _, _, landed, sem, dev = self.event(c, fam, ev)
            self.copies.arrived(landed, sem, dev)

    def stage(self, c, s):
        z_sem, z_dev = self.base[c] + 2 * N_EVENTS, (self.p.partner, self.p.t)
        if s < 2:
            local = pltpu.make_async_copy(self.own(c), self.bufs[c].at[self.p.tm], self.local_sems.at[c])
        if s == 0:
            self.copies.start(self.theirs(c), self.bufs[c].at[self.p.tm], z_sem, z_dev)
            self.start(c, 0, 0, 1, 4, 5)
            local.start()
        elif s == 1:
            self.copies.arrived(self.bufs[c].at[self.p.partner], z_sem, z_dev)
            self.start(c, 1, 0, 1, 4, 5)
            local.wait()
        else:
            for fam in range(2):
                if s == 2:
                    self.wait(c, fam, 0)
                    self.start(c, fam, 2, 8, 9)
                    self.wait(c, fam, 1)
                    self.start(c, fam, 3, 12, 13)
                    for ev in (4, 5):
                        self.wait(c, fam, ev)
                        self.start(c, fam, ev + 2)
                elif s == 3:
                    self.wait(c, fam, 2, 3)
                    self.start(c, fam, 16, 17)
                    for ev in (8, 9, 12, 13):
                        self.wait(c, fam, ev)
                        self.start(c, fam, ev + 2)
                elif s == 4:
                    for ev in (16, 17):
                        self.wait(c, fam, ev)
                        self.start(c, fam, ev + 2)
                else:
                    self.wait(c, fam, 6, 7, 10, 11, 14, 15, 18, 19)

    def tick(self, now):
        for c in range(5):
            if 0 <= now - START[c] < 6:
                self.stage(c, now - START[c])


class ZRing:
    def __init__(self, place, copies, buf):
        self.p, self.copies, self.buf = place, copies, buf
        self.base = copies.take(8)
        self.cut = buf.shape[2] // 2

    def slot(self, dz, other=0):
        c = self.p.c if other == 0 else 1 - self.p.c
        return ((self.p.z + dz + 4) % 4) * 2 + c

    def part(self, dz, half, other=0):
        s = self.slot(dz, other)
        if half is None:
            return self.buf.at[s]
        return self.buf.at[s, :, pl.ds(half * self.cut, self.cut)]

    EVENTS = ((0, None, 0), (0, None, 1), (0, None, -1), (-1, 0, 1), (-1, None, 0), (1, 1, -1), (1, None, 0), (2, None, 0))

    def start(self, *events):
        for ev in events:
            dz, half, way = self.EVENTS[ev]
            part = self.part(dz, half)
            dev = self.p.ring(way, self.p.c) if way else (self.p.tm, self.p.t + 1 - 2 * self.p.c)
            self.copies.start(part, part, self.base + ev, dev)

    def wait(self, *events):
        for ev in events:
            dz, half, way = self.EVENTS[ev]
            landed = self.part(dz - way, half) if way else self.part(dz, None, 1)
            dev = self.p.ring(way, self.p.c) if way else (self.p.tm, self.p.t + 1 - 2 * self.p.c)
            self.copies.arrived(landed, self.base + ev, dev)

    def first(self):
        self.start(0, 1, 2)

    def second(self):
        self.wait(1)
        self.start(3, 4)
        self.wait(2)
        self.start(5, 6)

    def third(self):
        self.wait(3, 5)
        self.start(7)


def dot(a, b):
    return jnp.dot(a, b, preferred_element_type=F32)


def nt_dot(a, b):
    return lax.dot_general(a, b, (((1,), (1,)), ((), ())), preferred_element_type=F32)


def iota(shape, dim):
    return lax.broadcasted_iota(jnp.int32, shape, dim)


def layer_kernel(
    frames, gain_attn, gain_mlp, bias, meta, w0, w1, w2, w3, w4, out,
    b0, b1, b2, b3, b4, spread, halo, wide, q_s, k_s, v_s, mix, mix_in, z_out, z_in, kept, stream,
    hid, pp, pp_in, ps, pr, own_sum, pall, outbox, meta_all,
    send_sems, recv_sems, local_sems, a2a_send, a2a_recv,
):
    p = Place()
    copies = Copies(send_sems, recv_sems)
    weights = RingGather(p, copies, (w0, w1, w2, w3, w4), (b0, b1, b2, b3, b4), local_sems)
    mate = (p.tm, p.t + 1 - 2 * p.c)

    def full(ref):
        return ref[...].reshape(DP, ref.shape[2])

    sem = pltpu.get_barrier_semaphore()
    cross = (1 - p.zl) * 2 + p.c

    @pl.loop(1, N_TM)
    def _(k):
        pl.semaphore_signal(sem, inc=1, device_id=((p.tm + k) % N_TM, p.t), device_id_type=MESH)

    for k in range(1, 4):
        for tm in (p.tm, p.partner):
            pl.semaphore_signal(sem, inc=1, device_id=(tm, (p.t + k) % 4), device_id_type=MESH)
    pl.semaphore_signal(
        sem, inc=1, device_id=((p.tm + 2 * p.zh - 1 + N_TM) % N_TM, cross), device_id_type=MESH
    )
    pl.semaphore_wait(sem, N_TM - 1 + 7)

    weights.tick(0)
    rows_c = pl.ds(pl.multiple_of(p.c * 128, 128), 128)
    rows_o = pl.ds(pl.multiple_of((1 - p.c) * 128, 128), 128)
    halo_sem = copies.take(4)
    below, above = ((p.tm + N_TM - 1) % N_TM, cross), ((p.tm + 1) % N_TM, cross)
    copies.start(frames.at[pl.ds(pl.multiple_of(p.c * 128, 128), 128)], halo.at[1, rows_c], halo_sem, below)
    copies.start(
        frames.at[pl.ds(pl.multiple_of(PATCHES + p.c * 128, 128), 128)], halo.at[0, rows_c], halo_sem + 1, above
    )
    meta_sem = copies.take()
    copies.start(meta, meta_all.at[p.zh], meta_sem, (p.partner, p.t))
    meta_all[p.zh] = meta[...]

    col = iota((1, DP), 1)
    target = jnp.where(col % PROWS < ROWS, col // PROWS * ROWS + col % PROWS, -1)

    @pl.loop(0, D // 128)
    def _(i):
        at = pl.ds(pl.multiple_of(i * 128, 128), 128)
        spread[at, :] = (iota((128, DP), 0) + i * 128 == target).astype(F32).astype(BF16)

    def norm_rows(values):
        values = values.astype(F32)
        centred = values - jnp.sum(values, axis=-1, keepdims=True) * (1.0 / D)
        var = jnp.sum(centred * centred, axis=-1, keepdims=True) * (1.0 / D)
        normed = (centred * lax.rsqrt(var + eps) * gain_attn[...]).astype(BF16)
        return dot(normed, spread[...]).astype(BF16)

    weights.tick(1)

    @pl.loop(0, 4)
    def _(i):
        at = pl.ds(pl.multiple_of(i * 128, 128), 128)
        wide[pl.ds(pl.multiple_of(PATCHES + i * 128, 128), 128), :] = norm_rows(frames[at, :])

    weights.tick(2)
    for i, dev in ((1, below), (0, above)):
        copies.arrived(halo.at[i, rows_c], halo_sem + 1 - i, dev)
        copies.start(halo.at[i, rows_c], halo.at[i, rows_c], halo_sem + 2 + i, mate)
    weights.tick(3)
    for i in range(2):
        copies.arrived(halo.at[i, rows_o], halo_sem + 2 + i, mate)

        @pl.loop(0, 2)
        def _(j, i=i):
            at = pl.ds(pl.multiple_of(j * 128, 128), 128)
            wide[pl.ds(pl.multiple_of(i * 3 * PATCHES + j * 128, 128), 128), :] = norm_rows(halo[i, at, :])

    for f in range(2):
        at = pl.ds(pl.multiple_of(f * PATCHES + p.t * BLK, BLK), BLK)
        stream[pl.ds(f * BLK, BLK), :] = dot(frames[at, :], spread[...])
    weights.tick(4)
    weights.tick(5)

    @pl.loop(0, 4)
    def _(i):
        at = pl.ds(pl.multiple_of(i * PATCHES, PATCHES), PATCHES)
        k_s[at, :] = dot(wide[at, :], b0[:, :, pl.ds(HW, HW)].reshape(DP, HW)).astype(BF16)
        v_s[at, :] = dot(wide[at, :], b0[:, :, pl.ds(2 * HW, HW)].reshape(DP, HW)).astype(BF16)

    @pl.loop(0, 2)
    def _(i):
        at = pl.ds(pl.multiple_of(i * PATCHES, PATCHES), PATCHES)
        src = pl.ds(pl.multiple_of((i + 1) * PATCHES, PATCHES), PATCHES)
        q_s[at, :] = dot(wide[src, :], b0[:, :, pl.ds(0, HW)].reshape(DP, HW)).astype(BF16)

    weights.tick(6)

    mix_sem = copies.take(6)
    scale = HEAD_DIM ** (-0.5)

    def attend(f):
        bias_rows = jnp.concatenate(
            [jnp.broadcast_to(bias[pl.ds(4 * f + b, 1), :], (BLK, 3 * PATCHES)) for b in range(4)], axis=0
        )
        keys = pl.ds(f * PATCHES, 3 * PATCHES)
        pieces = [jnp.zeros((PATCHES, 128), F32) for _ in range(3)]
        for h in range(HERE):
            lo, hi = h * HEAD_DIM, (h + 1) * HEAD_DIM
            first, last = lo // 128, (hi - 1) // 128
            n = (last - first + 1) * 128
            lanes = pl.ds(first * 128, n)
            lane = iota((PATCHES, n), 1) + first * 128
            mine = (lane >= lo) & (lane < hi)
            query = q_s[pl.ds(f * PATCHES, PATCHES), lanes].astype(F32)
            query = jnp.where(mine, query, 0.0).astype(BF16)
            scores = nt_dot(query, k_s[keys, lanes]) * scale + bias_rows
            expw = jnp.exp(scores - jnp.max(scores, axis=-1, keepdims=True))
            probs = (expw * (1.0 / jnp.sum(expw, axis=-1, keepdims=True))).astype(BF16)
            got = jnp.where(mine, dot(probs, v_s[keys, lanes]), 0.0)
            for j in range(first, last + 1):
                pieces[j] = pieces[j] + got[:, (j - first) * 128:(j - first + 1) * 128]
        attended = jnp.concatenate(pieces, axis=1).astype(BF16)
        return attended

    def mix_out(f, attended):
        for b in range(4):
            mix[f, b] = nt_dot(attended[b * BLK:(b + 1) * BLK], full(b1)).astype(BF16)
        for j in range(2):
            copies.start(mix.at[f, 2 * j + 1 - p.c], mix_in.at[f, j], mix_sem + 3 * f + j, mate)

    z_mate = (p.tm, (p.t + 2) % 4)

    def mix_sum(f):
        for j in range(2):
            copies.arrived(mix_in.at[f, j], mix_sem + 3 * f + j, mate)
        far = 1 - p.zl
        z_out[f] = (mix[f, 2 * far + p.c].astype(F32) + mix_in[f, far].astype(F32)).astype(BF16)
        copies.start(z_out.at[f], z_in.at[f], mix_sem + 3 * f + 2, z_mate)
        kept[f] = mix[f, 2 * p.zl + p.c].astype(F32) + mix_in[f, p.zl].astype(F32)

    attended = attend(0)
    weights.tick(7)
    mix_out(0, attended)
    attended = attend(1)
    mix_sum(0)
    weights.tick(8)
    mix_out(1, attended)
    weights.tick(9)
    mix_sum(1)

    hidden = ZRing(p, copies, hid)
    real = (col % PROWS < ROWS).astype(F32)
    for f in range(2):
        at = pl.ds(f * BLK, BLK)
        copies.arrived(z_in.at[f], mix_sem + 3 * f + 2, z_mate)
        rows = stream[at, :] + (kept[f] + z_in[f].astype(F32))
        stream[at, :] = rows
        centred = (rows - jnp.sum(rows, axis=-1, keepdims=True) * (1.0 / D)) * real
        var = jnp.sum(centred * centred, axis=-1, keepdims=True) * (1.0 / D)
        hid[hidden.slot(0), pl.ds(f * BLK, BLK), :] = (centred * lax.rsqrt(var + eps) * gain_mlp[...]).astype(BF16)
    hidden.first()
    copies.arrived(meta_all.at[1 - p.zh], meta_sem, (p.partner, p.t))
    weights.tick(10)
    weights.tick(11)

    part_sem = copies.take(4)
    ring_sem = copies.take(3)

    def chooser(zh, t):
        ids = meta_all[zh, pl.ds(t, 1), :]
        row, lane = iota((32, 128), 0), iota((32, 128), 1)
        return (jnp.broadcast_to(ids, (32, 128)) == row % 16) & (row // 16 == lane // BLK)

    def mlp(dz):
        z = (p.z + dz + 4) % 4
        rows = hid[pl.ds(z * 2, 2)].reshape(256, DP)
        up = dot(rows, full(b2))
        act = (0.5 * up * (1.0 + lax.erf(up * (0.5 ** 0.5)))).astype(BF16)
        down = nt_dot(act, full(b3)).astype(BF16)
        for c in range(2):
            choose = chooser(z // 2, (z % 2) * 2 + c).astype(F32).astype(BF16)
            pp[z, c] = dot(choose, down[c * 128:(c + 1) * 128]).astype(BF16)
        copies.start(pp.at[z, 1 - p.c], pp_in.at[z], part_sem + (dz + 1), mate)

    def pass_on(dz):
        z = (p.z + dz + 4) % 4
        copies.arrived(pp_in.at[z], part_sem + (dz + 1), mate)
        total = pp[z, p.c].astype(F32) + pp_in[z].astype(F32)
        if dz == 0:
            own_sum[...] = total
        else:
            k = {-1: 0, 1: 1, 2: 2}[dz]
            ps[k] = total.astype(BF16)
            copies.start(ps.at[k], pr.at[k], ring_sem + k, p.ring(dz, p.c))

    hidden.wait(0)
    mlp(0)
    hidden.second()
    weights.tick(12)
    pass_on(0)
    hidden.wait(4)
    mlp(-1)
    hidden.third()
    weights.tick(13)
    pass_on(-1)
    hidden.wait(6)
    mlp(1)
    pass_on(1)
    hidden.wait(7)
    mlp(2)
    pass_on(2)

    choose = chooser(p.zh, p.t).astype(F32)
    total = own_sum[...] + lax.dot_general(
        choose, stream[...], (((1,), (0,)), ((), ())), precision=lax.Precision.HIGHEST, preferred_element_type=F32
    )
    for k, dz in enumerate((-1, 1, 2)):
        copies.arrived(pr.at[k], ring_sem + k, p.ring(dz, p.c))
        total = total + pr[k].astype(F32)
    pooled = ZRing(p, copies, pall)
    pall[pooled.slot(0)] = (total * (1.0 / POOL)).astype(BF16)
    pooled.first()
    pooled.second()
    pooled.third()
    pooled.wait(0, 4, 6, 7)

    projected = dot(pall[...].reshape(256, DP), full(b4)).astype(BF16)
    for zh in range(2):
        dest = jnp.broadcast_to(meta_all[zh, pl.ds(4, 1), :], (256, 128))
        place = (iota((256, 128), 0) == dest).astype(F32).astype(BF16)
        slots = dot(place, projected[zh * 128:(zh + 1) * 128])
        outbox[:, zh] = slots.reshape(N_TM, 8, LM8).astype(BF16)

    def a2a(k, dst_tm, src_tm):
        cols = pl.ds(pl.multiple_of((src_tm % 2) * LM8, LM8), LM8)
        return pltpu.make_async_remote_copy(
            src_ref=outbox.at[dst_tm], dst_ref=out.at[src_tm // 2, :, :, cols],
            send_sem=a2a_send.at[k], recv_sem=a2a_recv.at[k],
            device_id=(dst_tm, p.t), device_id_type=MESH,
        )

    @pl.loop(1, N_TM)
    def _(k):
        a2a(k, (p.tm + k) % N_TM, p.tm).start()

    out[p.xy, :, :, pl.ds(pl.multiple_of(p.zh * LM8, LM8), LM8)] = outbox[p.tm]
    copies.drain()

    @pl.loop(1, N_TM)
    def _(k):
        a2a(k, (p.tm + k) % N_TM, (p.tm + N_TM - k) % N_TM).wait_recv()

    @pl.loop(1, N_TM)
    def _(k):
        a2a(k, (p.tm + k) % N_TM, p.tm).wait_send()


def layer(frames, gain_attn, gain_mlp, bias, meta, parts):
    vmem = pl.BlockSpec(memory_space=pltpu.VMEM)
    n_sems = 5 * (2 * N_EVENTS + 1) + 4 + 1 + 6 + 8 + 4 + 3 + 8
    V = pltpu.VMEM
    return pl.pallas_call(
        layer_kernel,
        out_shape=jax.ShapeDtypeStruct((N_TM // 2, 2, 8, 2 * LM8), BF16),
        in_specs=[vmem] * 10,
        out_specs=vmem,
        scratch_shapes=[V((N_TM, PROWS, n), BF16) for n in WIDTHS] + [
            V((D, DP), BF16),
            V((2, PATCHES, D), BF16),
            V((4 * PATCHES, DP), BF16),
            V((2 * PATCHES, HW), BF16),
            V((4 * PATCHES, HW), BF16),
            V((4 * PATCHES, HW), BF16),
            V((2, 4, BLK, DP), BF16),
            V((2, 2, BLK, DP), BF16),
            V((2, BLK, DP), BF16),
            V((2, BLK, DP), BF16),
            V((2, BLK, DP), F32),
            V((2 * BLK, DP), F32),
            V((8, 2 * BLK, DP), BF16),
            V((4, 2, 32, DP), BF16),
            V((4, 32, DP), BF16),
            V((3, 32, DP), BF16),
            V((3, 32, DP), BF16),
            V((32, DP), F32),
            V((8, 32, DP), BF16),
            V((N_TM, 2, 8, LM8), BF16),
            V((2, 8, 128), jnp.int32),
            pltpu.SemaphoreType.DMA((n_sems,)),
            pltpu.SemaphoreType.DMA((n_sems,)),
            pltpu.SemaphoreType.DMA((5,)),
            pltpu.SemaphoreType.DMA((N_TM,)),
            pltpu.SemaphoreType.DMA((N_TM,)),
        ],
        compiler_params=pltpu.CompilerParams(collective_id=0, has_side_effects=True, vmem_limit_bytes=60 << 20),
    )(frames, gain_attn, gain_mlp, bias, meta, *parts)


def body(
    frames, gain_attn, w_qkv, w_out, gain_mlp, w_up, w_down, w_proj, windows, pool_map, owners
):
    tm = lax.axis_index("tm")
    rows = ((0, PROWS - ROWS),)

    def halves(w):
        w = w.reshape(ROWS, 2, w.shape[1] // 2).transpose(1, 0, 2)
        return jnp.pad(w, ((0, 0),) + rows + ((0, 0),))

    parts = [
        jnp.pad(w_qkv, rows + ((0, 0), (0, HW - HERE * HEAD_DIM))).reshape(PROWS, 3 * HW),
        jnp.pad(w_out.T, rows + ((0, HW - HERE * HEAD_DIM),)),
        halves(w_up),
        halves(w_down.T),
        halves(w_proj),
    ]
    block = jnp.arange(8, dtype=jnp.int32)
    local = windows - tm * 8 + 4 - (block // 4 * 4)[:, None]
    key_block = jnp.arange(3 * PATCHES, dtype=jnp.int32) // BLK
    chosen = jnp.any(local[:, :, None] == key_block[None, None, :], axis=1)
    bias = jnp.where(chosen, 0.0, -1e30).astype(F32)
    ids = owners[:, 0]
    earlier = jnp.arange(128, dtype=jnp.int32)
    rank = jnp.sum(
        ((ids[:, None] == ids[None, :]) & (earlier[None, :] < earlier[:, None])).astype(jnp.int32), axis=1
    )
    dest = (ids * 8 + rank).reshape(2, 4, 16).transpose(1, 0, 2).reshape(1, 128)
    maps = pool_map.reshape(2, 4, BLK).transpose(1, 0, 2).reshape(4, 128)
    meta = jnp.concatenate([maps, dest, jnp.zeros((3, 128), jnp.int32)], axis=0)
    gain_wide = jnp.pad(gain_mlp.reshape(N_TM, ROWS), ((0, 0), (0, PROWS - ROWS))).reshape(1, DP)
    received = layer(frames, gain_attn.reshape(1, D), gain_wide, bias, meta, parts)
    return received.reshape(1, N_TM * 8, 2 * LM8)


def solution(mesh):
    placed = (
        P("tm", None),
        P(),
        P("tm", None, "tensor"),
        P("tensor", "tm"),
        P(),
        P("tm", "tensor"),
        P("tensor", "tm"),
        P("tm", "tensor"),
        P("tm", None),
        P("tm"),
        P("tm", None),
    )
    return jax.shard_map(
        body, mesh=mesh, in_specs=placed, out_specs=P("tm", None, "tensor"), check_vma=False
    )
```

time: 649 us -> 142 us (0.22)
  waiting for transfers between devices: 384 us -> 0 us
  blocking collectives: 125 us -> 0 us
  Pallas kernels: 0 us -> 124 us
  local copies, waits for them, and re-layouts: 75.8 us -> 12 us
  matrix products: 31.7 us -> 0 us
  between operations: 13.7 us -> 0.09 us
  other arithmetic: 13.3 us -> 3.76 us
    all_gather x4 -> x0, waiting for transfers between devices: 300 us -> none  [the longest x1 86.1 us: body(): lax.all_gather(w_up, 'tm', axis=0, tiled=True)]
    pallas_call x0 -> x1, Pallas kernels: none -> 124 us  [layer(): pl.pallas_call(layer_kernel, out_shape=jax.ShapeDtypeStruct((N_TM // 2, 2...]
    all_gather x1 -> x0, blocking collectives: 102 us -> none  [body(): lax.all_gather(w_out, 'tm', axis=1, tiled=True)]
    psum x2 -> x0, waiting for transfers between devices: 82 us -> none  [tensor_total(): return lax.psum(term.astype(jnp.bfloat16), 'tensor').astype(jnp.float32)]
    unnamed x31 -> x7, local copies, waits for them, and re-layouts: 38.5 us -> 3.48 us
    dot_general x7 -> x0, matrix products: 31.7 us -> none  [the longest x1 15.1 us: body(): jnp.dot(activation, full_down, preferred_element_type=jnp.float32)]
    all_to_all x1 -> x0, blocking collectives: 23.1 us -> none  [body(): lax.all_to_all(outbox, 'tm', split_axis=0, concat_axis=0, tiled=True)]
    gather x2 -> x0, local copies, waits for them, and re-layouts: 14.9 us -> none  [attend_group(): kv_blocks[id_group].reshape(group_size, WIN * BLK, 2, heads_here, head_dim)]
  transfers between devices with their start and end apart: 8 -> 0, of which waited for: 6 -> 0; matrix products, arithmetic and copies ran while one was open for 7% -> 0% of each run, Pallas kernels for 0% -> 0%
where the time goes in v2:
time: 142 us; the launch traced here: 140 us
  Pallas kernels  124 us (87%)
  local copies, waits for them, and re-layouts  12 us (8%)
  other arithmetic  3.76 us (3%)
    pallas_call x1, Pallas kernels, layer(): pl.pallas_call(layer_kernel, out_shape=jax.ShapeDtypeStruct((N_TM // 2, 2...  124 us
    unnamed x7, local copies, waits for them, and re-layouts  3.48 us

profile of v2, /device:TPU:0, one launch (start us, length us, event | category | flops | bytes accessed | tf_op | source)
XLA Modules:
  0.0 139.6 jit_solution(36592265346424879)
XLA Ops:
  0.0 0.9 convert_reduce_fusion
  0.9 0.7 multiply_reduce_fusion
  1.6 0.1 pad.31.clone
  1.7 0.8 add_subtract_fusion
  2.4 0.1 mul.24
  2.5 0.1 reduce_sum.12
  2.6 0.1 reshape.72
  2.7 0.8 reshape.70
  3.5 0.1 reshape.71
  3.6 0.7 add_add_fusion.meta
  4.2 0.1 compare_reduce_fusion
  4.4 1.3 reshape.67.gain_attn
  5.7 0.8 reshape.68
  6.5 0.7 reshape.69.gain_mlp
  7.1 0.6 broadcast_select_fusion.bias
  7.8 1.4 pad.25.w1
  9.1 0.9 reshape.76
  10.1 0.6 pad.28.w4
  10.7 0.9 copy.26
  11.8 0.7 copy.27
  12.5 0.7 pad.26.w2
  13.2 0.7 pad.27.w3
  13.9 123.8 %shard_map.109 = bf16[16,2,8,1024]{3,2,1,0:T(8,128)(2,1)} custom-call(bf16[512,1408]{1,0:T(8,128)(2,1)} %frames.1, f32[1,1408]{1,0:T(1,128)} %reshape.67.gain_attn, f32[1,1536]{1,0:T(1,128)} %reshape.69.gain_mlp, f32[8,768]{1,0:T(8,128)} %broadcast_select_fusion.bias, s32[8,128]{1,0:T(8,128)} %add_add_fusion.meta, bf16[48,1152]{1,0:T(8,128)(2,1)} %bitcast.22, ...), custom_call_target="tpu_custom_call" | custom-call | tf_op jit(solution)/shard_map/pallas_call | solution.py:498
  137.8 1.9 %copy.35 = bf16[1,256,1024]{2,1,0:T(8,128)(2,1)} copy(bf16[1,256,1024]{2,1,0:T(8,128)(2,1)} %bitcast.18) | data formatting | bytes 1048576
  (17 shorter events, 0.2 us)
Async XLA Ops:
  0.0 13.2 %copy-start.1 = (bf16[1536,44]{0,1:T(8,128)(2,1)S(1)}, bf16[1536,44]{0,1:T(8,128)(2,1)}, u32[]{:S(2)}) copy-start(bf16[1536,44]{0,1:T(8,128)(2,1)} %param.17) | copy-start | bytes 405508
  0.0 12.4 %copy-start = (bf16[44,1536]{1,0:T(8,128)(2,1)S(1)}, bf16[44,1536]{1,0:T(8,128)(2,1)}, u32[]{:S(2)}) copy-start(bf16[44,1536]{1,0:T(8,128)(2,1)} %param.16) | copy-start | bytes 405508

commit v3 on v2

--- a/solution.py
+++ b/solution.py
@@ -25,6 +25,7 @@
 WIDTHS = (3 * HW, HW, FF8, FF8, LM8)
 QKV, OUT, UP, DOWN, PROJ = range(5)
 START = (0, 2, 4, 6, 8)
+BANDS = (0, 128, 384, 640, 896, 1024)
 
 eps = 1e-06
 MESH = pl.DeviceIdType.MESH
@@ -177,8 +178,9 @@
 
 
 class ZRing:
-    def __init__(self, place, copies, buf):
+    def __init__(self, place, copies, buf, first, count):
         self.p, self.copies, self.buf = place, copies, buf
+        self.rows = pl.ds(first, count)
         self.base = copies.take(8)
         self.cut = buf.shape[2] // 2
 
@@ -189,8 +191,8 @@
     def part(self, dz, half, other=0):
         s = self.slot(dz, other)
         if half is None:
-            return self.buf.at[s]
-        return self.buf.at[s, :, pl.ds(half * self.cut, self.cut)]
+            return self.buf.at[s, self.rows]
+        return self.buf.at[s, self.rows, pl.ds(half * self.cut, self.cut)]
 
     EVENTS = ((0, None, 0), (0, None, 1), (0, None, -1), (-1, 0, 1), (-1, None, 0), (1, 1, -1), (1, None, 0), (2, None, 0))
 
@@ -235,14 +237,14 @@
 
 
 def layer_kernel(
-    frames, gain_attn, gain_mlp, bias, meta, w0, w1, w2, w3, w4, out,
-    b0, b1, b2, b3, b4, spread, halo, wide, q_s, k_s, v_s, mix, mix_in, z_out, z_in, kept, stream,
-    hid, pp, pp_in, ps, pr, own_sum, pall, outbox, meta_all,
+    frames, gain_attn, gain_mlp, windows, pool_map, owners, w_qkv, w_out_t, w_up, w_down_t, w_proj, out,
+    s0, s1, s2, s3, s4, b0, b1, b2, b3, b4, band, halo, wide, q_s, k_s, v_s, mix, mix_in, z_out, z_in, kept, stream,
+    hid, pp, pp_in, ps, pr, own_sum, pall, outbox, meta, meta_all, bias, gain_row, gain_wide,
     send_sems, recv_sems, local_sems, a2a_send, a2a_recv,
 ):
     p = Place()
     copies = Copies(send_sems, recv_sems)
-    weights = RingGather(p, copies, (w0, w1, w2, w3, w4), (b0, b1, b2, b3, b4), local_sems)
+    weights = RingGather(p, copies, (s0, s1, s2, s3, s4), (b0, b1, b2, b3, b4), local_sems)
     mate = (p.tm, p.t + 1 - 2 * p.c)
 
     def full(ref):
@@ -250,86 +252,131 @@
 
     sem = pltpu.get_barrier_semaphore()
     cross = (1 - p.zl) * 2 + p.c
-
-    @pl.loop(1, N_TM)
-    def _(k):
-        pl.semaphore_signal(sem, inc=1, device_id=((p.tm + k) % N_TM, p.t), device_id_type=MESH)
-
-    for k in range(1, 4):
-        for tm in (p.tm, p.partner):
-            pl.semaphore_signal(sem, inc=1, device_id=(tm, (p.t + k) % 4), device_id_type=MESH)
-    pl.semaphore_signal(
-        sem, inc=1, device_id=((p.tm + 2 * p.zh - 1 + N_TM) % N_TM, cross), device_id_type=MESH
-    )
-    pl.semaphore_wait(sem, N_TM - 1 + 7)
-
+    greeted = [(weights.at(0, a, b, p.zh), p.t) for a, b in ((1, 0), (-1, 0), (0, 1), (0, -1))]
+    greeted += [(p.partner, p.t)]
+    greeted += [(tm, (p.t + k) % 4) for k in range(1, 4) for tm in (p.tm, p.partner)]
+    greeted += [((p.tm + 2 * p.zh - 1 + N_TM) % N_TM, cross)]
+    for dev in greeted:
+        pl.semaphore_signal(sem, inc=1, device_id=dev, device_id_type=MESH)
+
+    wide_here = HERE * HEAD_DIM
+    s0[...] = jnp.zeros((PROWS, 3 * HW), BF16)
+    for j in range(3):
+        s0[0:ROWS, j * HW:j * HW + wide_here] = w_qkv[j]
+    pl.semaphore_wait(sem, len(greeted))
     weights.tick(0)
+    s1[...] = jnp.zeros((PROWS, HW), BF16)
+    s1[0:ROWS, 0:wide_here] = w_out_t[...]
+    for st, w in ((s2, w_up), (s3, w_down_t), (s4, w_proj)):
+        n = st.shape[2]
+        for h in range(2):
+            st[h] = jnp.zeros((PROWS, n), BF16)
+            st[h, 0:ROWS, :] = w[:, h * n:(h + 1) * n]
+
+    for j, first in enumerate(BANDS):
+        col = iota((1, 256), 1) + j * 256
+        target = jnp.where(col % PROWS < ROWS, col // PROWS * ROWS + col % PROWS, -1)
+        band[j] = (iota((384, 256), 0) + first == target).astype(F32).astype(BF16)
+
+    def spread(values):
+        return jnp.concatenate(
+            [dot(values[:, first:first + 384], band[j]) for j, first in enumerate(BANDS)], axis=1
+        )
+
+    gain_row[...] = jnp.concatenate([gain_attn[i:i + 1, :] for i in range(D // 128)], axis=1)
+
+    def norm_rows(values):
+        values = values.astype(F32)
+        centred = values - jnp.sum(values, axis=-1, keepdims=True) * (1.0 / D)
+        var = jnp.sum(centred * centred, axis=-1, keepdims=True) * (1.0 / D)
+        normed = (centred * lax.rsqrt(var + eps) * gain_row[...]).astype(BF16)
+        return spread(normed).astype(BF16)
+
+    weights.tick(1)
+
+    part = jnp.concatenate([gain_mlp[i:i + 1, :] for i in range(D // 128)], axis=1)
+    gain = jnp.zeros((1, DP), F32)
+    for _ in range(3):
+        top = part.astype(BF16)
+        gain = gain + spread(jnp.broadcast_to(top.astype(F32), (16, D)).astype(BF16))[0:1]
+        part = part - top.astype(F32)
+    gain_wide[...] = gain
+
+    block = iota((8, 3 * PATCHES), 0)
+    key_block = iota((8, 3 * PATCHES), 1) // BLK + p.tm * 8 - 4 + block // 4 * 4
+    hits = jnp.zeros((8, 3 * PATCHES), jnp.int32)
+    for j in range(WIN):
+        hits = hits + (jnp.broadcast_to(windows[:, j:j + 1], (8, 3 * PATCHES)) == key_block).astype(jnp.int32)
+    bias[...] = jnp.where(hits > 0, 0.0, -1e30).astype(F32)
+
+    lane = iota((1, 128), 1)
+    meta[...] = jnp.zeros((8, 128), jnp.int32)
+    for t in range(4):
+        f0, f1 = pool_map[t // 2:t // 2 + 1, :], pool_map[2 + t // 2:3 + t // 2, :]
+        if t % 2 == 0:
+            f1 = jnp.concatenate([f1[:, BLK:], f1[:, :BLK]], axis=1)
+        else:
+            f0 = jnp.concatenate([f0[:, BLK:], f0[:, :BLK]], axis=1)
+        meta[t:t + 1, :] = jnp.where(lane < BLK, f0, f1)
+
+    def natural(i):
+        return (i // 16) % 2 * 64 + i // 32 * 16 + i % 16
+
+    to, at_row = natural(iota((128, 128), 1)), iota((128, 128), 0)
+    ids = jnp.broadcast_to(owners[...], (16, 128)).astype(F32).astype(BF16)
+    ids = dot(ids, (at_row == to).astype(F32).astype(BF16))[0:1]
+    wide_ids = jnp.broadcast_to(ids, (128, 128))
+    before = (jnp.transpose(wide_ids) == wide_ids) & (natural(at_row) < to)
+    rank = jnp.sum(before.astype(F32), axis=0, keepdims=True)
+    meta[4:5, :] = (ids * 8.0 + rank).astype(jnp.int32)
+    meta_sem = copies.take()
+    meta_all[p.zh] = meta[...]
+
     rows_c = pl.ds(pl.multiple_of(p.c * 128, 128), 128)
     rows_o = pl.ds(pl.multiple_of((1 - p.c) * 128, 128), 128)
     halo_sem = copies.take(4)
     below, above = ((p.tm + N_TM - 1) % N_TM, cross), ((p.tm + 1) % N_TM, cross)
+    weights.tick(2)
     copies.start(frames.at[pl.ds(pl.multiple_of(p.c * 128, 128), 128)], halo.at[1, rows_c], halo_sem, below)
     copies.start(
         frames.at[pl.ds(pl.multiple_of(PATCHES + p.c * 128, 128), 128)], halo.at[0, rows_c], halo_sem + 1, above
     )
-    meta_sem = copies.take()
+
+    def norm_own(i):
+        wide[pl.ds((i + 1) * PATCHES, PATCHES), :] = norm_rows(frames[pl.ds(i * PATCHES, PATCHES), :])
+
+    norm_own(0)
+    weights.tick(3)
+    norm_own(1)
     copies.start(meta, meta_all.at[p.zh], meta_sem, (p.partner, p.t))
-    meta_all[p.zh] = meta[...]
-
-    col = iota((1, DP), 1)
-    target = jnp.where(col % PROWS < ROWS, col // PROWS * ROWS + col % PROWS, -1)
-
-    @pl.loop(0, D // 128)
-    def _(i):
-        at = pl.ds(pl.multiple_of(i * 128, 128), 128)
-        spread[at, :] = (iota((128, DP), 0) + i * 128 == target).astype(F32).astype(BF16)
-
-    def norm_rows(values):
-        values = values.astype(F32)
-        centred = values - jnp.sum(values, axis=-1, keepdims=True) * (1.0 / D)
-        var = jnp.sum(centred * centred, axis=-1, keepdims=True) * (1.0 / D)
-        normed = (centred * lax.rsqrt(var + eps) * gain_attn[...]).astype(BF16)
-        return dot(normed, spread[...]).astype(BF16)
-
-    weights.tick(1)
-
-    @pl.loop(0, 4)
-    def _(i):
-        at = pl.ds(pl.multiple_of(i * 128, 128), 128)
-        wide[pl.ds(pl.multiple_of(PATCHES + i * 128, 128), 128), :] = norm_rows(frames[at, :])
-
-    weights.tick(2)
+    weights.tick(4)
+
+    for f in range(2):
+        at = pl.ds(pl.multiple_of(f * PATCHES + p.t * BLK, BLK), BLK)
+        stream[pl.ds(f * BLK, BLK), :] = spread(frames[at, :])
+    weights.tick(5)
+
+    own = dot(wide[pl.ds(PATCHES, 2 * PATCHES), :], full(b0)).astype(BF16)
+    q_s[...] = own[:, :HW]
+    k_s[pl.ds(PATCHES, 2 * PATCHES), :] = own[:, HW:2 * HW]
+    v_s[pl.ds(PATCHES, 2 * PATCHES), :] = own[:, 2 * HW:]
+    weights.tick(6)
     for i, dev in ((1, below), (0, above)):
         copies.arrived(halo.at[i, rows_c], halo_sem + 1 - i, dev)
         copies.start(halo.at[i, rows_c], halo.at[i, rows_c], halo_sem + 2 + i, mate)
-    weights.tick(3)
+    weights.tick(7)
     for i in range(2):
         copies.arrived(halo.at[i, rows_o], halo_sem + 2 + i, mate)
 
-        @pl.loop(0, 2)
-        def _(j, i=i):
-            at = pl.ds(pl.multiple_of(j * 128, 128), 128)
-            wide[pl.ds(pl.multiple_of(i * 3 * PATCHES + j * 128, 128), 128), :] = norm_rows(halo[i, at, :])
-
-    for f in range(2):
-        at = pl.ds(pl.multiple_of(f * PATCHES + p.t * BLK, BLK), BLK)
-        stream[pl.ds(f * BLK, BLK), :] = dot(frames[at, :], spread[...])
-    weights.tick(4)
-    weights.tick(5)
-
-    @pl.loop(0, 4)
-    def _(i):
-        at = pl.ds(pl.multiple_of(i * PATCHES, PATCHES), PATCHES)
-        k_s[at, :] = dot(wide[at, :], b0[:, :, pl.ds(HW, HW)].reshape(DP, HW)).astype(BF16)
-        v_s[at, :] = dot(wide[at, :], b0[:, :, pl.ds(2 * HW, HW)].reshape(DP, HW)).astype(BF16)
-
     @pl.loop(0, 2)
     def _(i):
-        at = pl.ds(pl.multiple_of(i * PATCHES, PATCHES), PATCHES)
-        src = pl.ds(pl.multiple_of((i + 1) * PATCHES, PATCHES), PATCHES)
-        q_s[at, :] = dot(wide[src, :], b0[:, :, pl.ds(0, HW)].reshape(DP, HW)).astype(BF16)
-
-    weights.tick(6)
+        at = pl.ds(pl.multiple_of(i * 3 * PATCHES, PATCHES), PATCHES)
+        normed = norm_rows(halo[i])
+        got = dot(normed, b0[:, :, pl.ds(HW, 2 * HW)].reshape(DP, 2 * HW)).astype(BF16)
+        k_s[at, :] = got[:, :HW]
+        v_s[at, :] = got[:, HW:]
+
+    weights.tick(8)
 
     mix_sem = copies.take(6)
     scale = HEAD_DIM ** (-0.5)
@@ -359,8 +406,9 @@
         return attended
 
     def mix_out(f, attended):
+        terms = nt_dot(attended, full(b1)).astype(BF16)
         for b in range(4):
-            mix[f, b] = nt_dot(attended[b * BLK:(b + 1) * BLK], full(b1)).astype(BF16)
+            mix[f, b] = terms[b * BLK:(b + 1) * BLK]
         for j in range(2):
             copies.start(mix.at[f, 2 * j + 1 - p.c], mix_in.at[f, j], mix_sem + 3 * f + j, mate)
 
@@ -374,30 +422,35 @@
         copies.start(z_out.at[f], z_in.at[f], mix_sem + 3 * f + 2, z_mate)
         kept[f] = mix[f, 2 * p.zl + p.c].astype(F32) + mix_in[f, p.zl].astype(F32)
 
-    attended = attend(0)
-    weights.tick(7)
-    mix_out(0, attended)
-    attended = attend(1)
-    mix_sum(0)
-    weights.tick(8)
-    mix_out(1, attended)
-    weights.tick(9)
-    mix_sum(1)
-
-    hidden = ZRing(p, copies, hid)
-    real = (col % PROWS < ROWS).astype(F32)
-    for f in range(2):
+    hidden = [ZRing(p, copies, hid, f * BLK, BLK) for f in range(2)]
+    column = iota((1, DP), 1)
+    real = (column % PROWS < ROWS).astype(F32)
+
+    def second_norm(f):
         at = pl.ds(f * BLK, BLK)
         copies.arrived(z_in.at[f], mix_sem + 3 * f + 2, z_mate)
         rows = stream[at, :] + (kept[f] + z_in[f].astype(F32))
         stream[at, :] = rows
         centred = (rows - jnp.sum(rows, axis=-1, keepdims=True) * (1.0 / D)) * real
         var = jnp.sum(centred * centred, axis=-1, keepdims=True) * (1.0 / D)
-        hid[hidden.slot(0), pl.ds(f * BLK, BLK), :] = (centred * lax.rsqrt(var + eps) * gain_mlp[...]).astype(BF16)
-    hidden.first()
+        normed = (centred * lax.rsqrt(var + eps) * gain_wide[...]).astype(BF16)
+        hid[hidden[f].slot(0), at, :] = normed
+        hidden[f].first()
+
+    mix_out(0, attend(0))
+    weights.tick(9)
+    mix_sum(0)
+    attended = attend(1)
+    weights.tick(10)
+    mix_out(1, attended)
+    second_norm(0)
+    mix_sum(1)
+    weights.tick(11)
+    hidden[0].second()
+    second_norm(1)
     copies.arrived(meta_all.at[1 - p.zh], meta_sem, (p.partner, p.t))
-    weights.tick(10)
-    weights.tick(11)
+    weights.tick(12)
+    hidden[0].third()
 
     part_sem = copies.take(4)
     ring_sem = copies.take(3)
@@ -429,20 +482,23 @@
             ps[k] = total.astype(BF16)
             copies.start(ps.at[k], pr.at[k], ring_sem + k, p.ring(dz, p.c))
 
-    hidden.wait(0)
+    for f in range(2):
+        hidden[f].wait(0)
     mlp(0)
-    hidden.second()
-    weights.tick(12)
+    hidden[1].second()
     pass_on(0)
-    hidden.wait(4)
+    for f in range(2):
+        hidden[f].wait(4)
     mlp(-1)
-    hidden.third()
+    hidden[1].third()
     weights.tick(13)
     pass_on(-1)
-    hidden.wait(6)
+    for f in range(2):
+        hidden[f].wait(6)
     mlp(1)
     pass_on(1)
-    hidden.wait(7)
+    for f in range(2):
+        hidden[f].wait(7)
     mlp(2)
     pass_on(2)
 
@@ -453,7 +509,7 @@
     for k, dz in enumerate((-1, 1, 2)):
         copies.arrived(pr.at[k], ring_sem + k, p.ring(dz, p.c))
         total = total + pr[k].astype(F32)
-    pooled = ZRing(p, copies, pall)
+    pooled = ZRing(p, copies, pall, 0, 32)
     pall[pooled.slot(0)] = (total * (1.0 / POOL)).astype(BF16)
     pooled.first()
     pooled.second()
@@ -491,19 +547,20 @@
         a2a(k, (p.tm + k) % N_TM, p.tm).wait_send()
 
 
-def layer(frames, gain_attn, gain_mlp, bias, meta, parts):
+def layer(*args):
     vmem = pl.BlockSpec(memory_space=pltpu.VMEM)
-    n_sems = 5 * (2 * N_EVENTS + 1) + 4 + 1 + 6 + 8 + 4 + 3 + 8
+    n_sems = 5 * (2 * N_EVENTS + 1) + 4 + 1 + 6 + 16 + 4 + 3 + 8
     V = pltpu.VMEM
+    staged = [V((PROWS, n), BF16) if i < UP else V((2, PROWS, n), BF16) for i, n in enumerate(WIDTHS)]
     return pl.pallas_call(
         layer_kernel,
         out_shape=jax.ShapeDtypeStruct((N_TM // 2, 2, 8, 2 * LM8), BF16),
-        in_specs=[vmem] * 10,
+        in_specs=[vmem] * len(args),
         out_specs=vmem,
-        scratch_shapes=[V((N_TM, PROWS, n), BF16) for n in WIDTHS] + [
-            V((D, DP), BF16),
+        scratch_shapes=staged + [V((N_TM, PROWS, n), BF16) for n in WIDTHS] + [
+            V((6, 384, 256), BF16),
             V((2, PATCHES, D), BF16),
-            V((4 * PATCHES, DP), BF16),
+            V((3 * PATCHES, DP), BF16),
             V((2 * PATCHES, HW), BF16),
             V((4 * PATCHES, HW), BF16),
             V((4 * PATCHES, HW), BF16),
@@ -521,7 +578,11 @@
             V((32, DP), F32),
             V((8, 32, DP), BF16),
             V((N_TM, 2, 8, LM8), BF16),
+            V((8, 128), jnp.int32),
             V((2, 8, 128), jnp.int32),
+            V((8, 3 * PATCHES), F32),
+            V((1, D), F32),
+            V((1, DP), F32),
             pltpu.SemaphoreType.DMA((n_sems,)),
             pltpu.SemaphoreType.DMA((n_sems,)),
             pltpu.SemaphoreType.DMA((5,)),
@@ -529,41 +590,17 @@
             pltpu.SemaphoreType.DMA((N_TM,)),
         ],
         compiler_params=pltpu.CompilerParams(collective_id=0, has_side_effects=True, vmem_limit_bytes=60 << 20),
-    )(frames, gain_attn, gain_mlp, bias, meta, *parts)
+    )(*args)
 
 
 def body(
     frames, gain_attn, w_qkv, w_out, gain_mlp, w_up, w_down, w_proj, windows, pool_map, owners
 ):
-    tm = lax.axis_index("tm")
-    rows = ((0, PROWS - ROWS),)
-
-    def halves(w):
-        w = w.reshape(ROWS, 2, w.shape[1] // 2).transpose(1, 0, 2)
-        return jnp.pad(w, ((0, 0),) + rows + ((0, 0),))
-
-    parts = [
-        jnp.pad(w_qkv, rows + ((0, 0), (0, HW - HERE * HEAD_DIM))).reshape(PROWS, 3 * HW),
-        jnp.pad(w_out.T, rows + ((0, HW - HERE * HEAD_DIM),)),
-        halves(w_up),
-        halves(w_down.T),
-        halves(w_proj),
-    ]
-    block = jnp.arange(8, dtype=jnp.int32)
-    local = windows - tm * 8 + 4 - (block // 4 * 4)[:, None]
-    key_block = jnp.arange(3 * PATCHES, dtype=jnp.int32) // BLK
-    chosen = jnp.any(local[:, :, None] == key_block[None, None, :], axis=1)
-    bias = jnp.where(chosen, 0.0, -1e30).astype(F32)
-    ids = owners[:, 0]
-    earlier = jnp.arange(128, dtype=jnp.int32)
-    rank = jnp.sum(
-        ((ids[:, None] == ids[None, :]) & (earlier[None, :] < earlier[:, None])).astype(jnp.int32), axis=1
+    received = layer(
+        frames, gain_attn.reshape(D // 128, 128), gain_mlp.reshape(D // 128, 128), windows,
+        pool_map.reshape(4, 128), owners.reshape(1, 128),
+        w_qkv.transpose(1, 0, 2), w_out.T, w_up, w_down.T, w_proj,
     )
-    dest = (ids * 8 + rank).reshape(2, 4, 16).transpose(1, 0, 2).reshape(1, 128)
-    maps = pool_map.reshape(2, 4, BLK).transpose(1, 0, 2).reshape(4, 128)
-    meta = jnp.concatenate([maps, dest, jnp.zeros((3, 128), jnp.int32)], axis=0)
-    gain_wide = jnp.pad(gain_mlp.reshape(N_TM, ROWS), ((0, 0), (0, PROWS - ROWS))).reshape(1, DP)
-    received = layer(frames, gain_attn.reshape(1, D), gain_wide, bias, meta, parts)
     return received.reshape(1, N_TM * 8, 2 * LM8)
 
 

time: 142 us -> 133 us (0.937)
  local copies, waits for them, and re-layouts: 12 us -> 1.87 us
  Pallas kernels: 124 us -> 129 us
  other arithmetic: 3.76 us -> 0 us
    pallas_call x1, Pallas kernels: 124 us -> 129 us  [layer(): pl.pallas_call(layer_kernel, out_shape=jax.ShapeDtypeStruct((N_TM // 2, 2...]
    reshape x12 -> x0, local copies, waits for them, and re-layouts: 4.77 us -> none  [the longest x1 1.29 us: body(): gain_attn.reshape(1, D)]
    pad x6 -> x0, local copies, waits for them, and re-layouts: 3.45 us -> none  [the longest x3 2 us: halves(): return jnp.pad(w, ((0, 0),) + rows + ((0, 0),))]
    unnamed x7 -> x1, local copies, waits for them, and re-layouts: 3.48 us -> 1.87 us
where the time goes in v3:
time: 133 us; the launch traced here: 131 us
  Pallas kernels  129 us (97%)
  local copies, waits for them, and re-layouts  1.87 us (1%)
    pallas_call x1, Pallas kernels, layer(): pl.pallas_call(layer_kernel, out_shape=jax.ShapeDtypeStruct((N_TM // 2, 2...  129 us

profile of v3, /device:TPU:0, one launch (start us, length us, event | category | flops | bytes accessed | tf_op | source)
XLA Modules:
  0.0 131.4 jit_solution(5643835526793973568)
XLA Ops:
  0.0 129.5 %shard_map.109 = bf16[16,2,8,1024]{3,2,1,0:T(8,128)(2,1)} custom-call(bf16[512,1408]{1,0:T(8,128)(2,1)} %frames.1, f32[11,128]{1,0:T(8,128)} %bitcast.12, f32[11,128]{1,0:T(8,128)} %bitcast.13, s32[8,8]{1,0:T(8,128)} %windows.1, s32[4,128]{1,0:T(4,128)} %bitcast.14, s32[1,128]{1,0:T(1,128)} %bitcast.15, bf16[3,44,352]{2,1,0:T(8,128)(2,1)} %bitcast.10, ...), custom_call_target="tpu_custom_call" | custom-call | tf_op jit(solution)/shard_map/pallas_call | solution.py:555
  129.5 1.9 %copy.13 = bf16[1,256,1024]{2,1,0:T(8,128)(2,1)} copy(bf16[1,256,1024]{2,1,0:T(8,128)(2,1)} %bitcast.8) | data formatting | bytes 1048576
